TPU v7x, 256 devices: a whole 4x4x8 slice. The times are simulated.
256 devices in a mesh: grp: 8 (over x, core), seq: 32 (over y, z).
Axes of the slice: x: 4, y: 4, z: 8, core: 2. Of those that a mesh axis runs over, the one named last changes fastest.
Arguments:
- query_rows: bfloat16 [8, 2, 2560, 4096], P('grp', None, 'seq'), may hold values from -5 to 5
- key_rows: bfloat16 [8, 2, 2560, 4096], P('grp', None, 'seq'), may hold values from -5 to 5
- value_rows: bfloat16 [8, 2, 2560, 4096], P('grp', None, 'seq'), may hold values from -6 to 6
- out_grad: bfloat16 [8, 2, 2560, 4096], P('grp', None, 'seq'), may hold values from -6 to 6
- lengths: int32 [8, 2], replicated, may hold values from 512 to 2560, as said below
Outputs:
- attended: bfloat16 [8, 2, 2560, 4096], P('grp', None, 'seq')
- query_grad: bfloat16 [8, 2, 2560, 4096], P('grp', None, 'seq')
- key_grad: bfloat16 [8, 2, 2560, 4096], P('grp', None, 'seq')
- value_grad: bfloat16 [8, 2, 2560, 4096], P('grp', None, 'seq')
Inputs may be any that keep to these rules, and one draw needn't show every extreme that they name: `lengths`: every length is a multiple of 128; in every draw some video has exactly 2560 tokens and some exactly 512.
All inputs are finite; a program needn't handle non-finite values.
Results may differ from a plain program's by a relative error of at most 0.02.
Values may be sent and summed in bfloat16 or wider, within the bound.
No kernel may reach another device: no remote copies, remote signals or barrier semaphores. Data moves between devices by JAX's collectives and lax.ppermute only.
A program may use at most 128 MiB of HBM per device.

v0:
```python
import jax
import jax.numpy as jnp
from jax import lax
from jax.sharding import PartitionSpec as P

HEADS = 32
HD = 128
MAX_LEN = 2560
TILE = 512


def partner(value, axis, bit):
    mask = 2**bit
    pairs = [(source, source ^ mask) for source in range(lax.axis_size(axis))]
    return lax.ppermute(value, axis, pairs)


def sent_together(arrays, axis, split_dim, concat_dim, along):
    ends, at = ([], 0)
    for a in arrays[:-1]:
        at += a.shape[along]
        ends.append(at)
    both = jnp.concatenate(arrays, axis=along)
    return tuple(
        jnp.split(
            lax.all_to_all(both, axis, split_axis=split_dim, concat_axis=concat_dim, tiled=True),
            ends,
            axis=along,
        )
    )


def tile_pass(data, length, base, start, tile, extent):
    scaling = HD ** (-0.5)
    query_tile = lax.dynamic_slice_in_dim(data[0], start, TILE, 0)
    grad_tile = lax.dynamic_slice_in_dim(data[3], start, TILE, 0)
    key_block = lax.dynamic_slice_in_dim(data[1], base, extent, 0)
    value_block = lax.dynamic_slice_in_dim(data[2], base, extent, 0)
    key_valid = jnp.arange(extent) < length
    row_valid = tile * TILE + jnp.arange(TILE) < length
    scores = (
        jnp.einsum("qhd,khd->hqk", query_tile, key_block, preferred_element_type=jnp.float32)
        * scaling
    )
    scores = jnp.where(key_valid[None, None, :], scores, -1e30)
    largest = jnp.max(scores, axis=2, keepdims=True)
    weights = jnp.exp(scores - largest)
    probs = weights / jnp.sum(weights, axis=2, keepdims=True)
    probs = jnp.where(row_valid[None, :, None], probs, 0.0)
    probs_half = probs.astype(jnp.bfloat16)
    output = jnp.einsum(
        "hqk,khd->qhd", probs_half, value_block, preferred_element_type=jnp.float32
    ).astype(jnp.bfloat16)
    delta = jnp.sum(grad_tile.astype(jnp.float32) * output.astype(jnp.float32), axis=2)
    grad_probs = jnp.einsum(
        "qhd,khd->hqk", grad_tile, value_block, preferred_element_type=jnp.float32
    )
    grad_scores = (probs * (grad_probs - delta.T[:, :, None])).astype(jnp.bfloat16)
    query_grad = (
        jnp.einsum("hqk,khd->qhd", grad_scores, key_block, preferred_element_type=jnp.float32)
        * scaling
    ).astype(jnp.bfloat16)
    key_part = (
        jnp.einsum("hqk,qhd->khd", grad_scores, query_tile, preferred_element_type=jnp.float32)
        * scaling
    )
    value_part = jnp.einsum(
        "hqk,qhd->khd", probs_half, grad_tile, preferred_element_type=jnp.float32
    )
    return (output, query_grad, key_part, value_part)


def run_tasks(data, lengths_pair, chosen, buffers):
    per_video = MAX_LEN // TILE

    def one_task(index, carry):
        video = index // per_video
        tile = index % per_video
        length = lengths_pair[video]
        base = video * MAX_LEN
        start = base + tile * TILE

        def make_branch(extent):

            def compute(state):
                out_buffer, qgrad_buffer, key_acc, value_acc = state
                output, query_grad, key_part, value_part = tile_pass(
                    data, length, base, start, tile, extent
                )
                out_buffer = lax.dynamic_update_slice_in_dim(out_buffer, output, start, 0)
                qgrad_buffer = lax.dynamic_update_slice_in_dim(qgrad_buffer, query_grad, start, 0)
                key_acc = lax.dynamic_update_slice_in_dim(
                    key_acc, lax.dynamic_slice_in_dim(key_acc, base, extent, 0) + key_part, base, 0
                )
                value_acc = lax.dynamic_update_slice_in_dim(
                    value_acc,
                    lax.dynamic_slice_in_dim(value_acc, base, extent, 0) + value_part,
                    base,
                    0,
                )
                return (out_buffer, qgrad_buffer, key_acc, value_acc)

            return compute

        branches = [make_branch(blocks * TILE) for blocks in range(1, per_video + 1)]
        needed = (length + TILE - 1) // TILE

        def working(state):
            return lax.switch(needed - 1, branches, state)

        def unchanged(state):
            return state

        return lax.cond(chosen[index], working, unchanged, carry)

    return lax.fori_loop(0, 2 * per_video, one_task, buffers)


def send_back(other_buffers, partner_bit):
    back_out, back_qgrad = partner((other_buffers[0], other_buffers[1]), "grp", partner_bit)
    back_key, back_value = partner((other_buffers[2], other_buffers[3]), "grp", partner_bit)
    return (back_out, back_qgrad, back_key, back_value)


def per_device(query_rows, key_rows, value_rows, out_grad, lengths):
    local_rows = query_rows.shape[2]
    query_split = query_rows.reshape(1, 2, local_rows, HEADS, HD)
    key_split = key_rows.reshape(1, 2, local_rows, HEADS, HD)
    value_split = value_rows.reshape(1, 2, local_rows, HEADS, HD)
    grad_split = out_grad.reshape(1, 2, local_rows, HEADS, HD)
    query_heads, key_heads, value_heads, grad_heads = (
        lax.all_to_all(query_split, "seq", split_axis=3, concat_axis=2, tiled=True),
        lax.all_to_all(key_split, "seq", split_axis=3, concat_axis=2, tiled=True),
        lax.all_to_all(value_split, "seq", split_axis=3, concat_axis=2, tiled=True),
        lax.all_to_all(grad_split, "seq", split_axis=3, concat_axis=2, tiled=True),
    )
    local_heads = query_heads.shape[3]
    own_data = tuple(
        (
            item.reshape(2 * MAX_LEN, local_heads, HD)
            for item in (query_heads, key_heads, value_heads, grad_heads)
        )
    )
    group = lax.axis_index("grp")
    own_lengths = lengths[group]
    per_video = MAX_LEN // TILE
    tile_ids = jnp.arange(2 * per_video) % per_video
    zero_half = jnp.zeros(own_data[0].shape, jnp.bfloat16)
    zero_full = jnp.zeros(own_data[0].shape, jnp.float32)
    start_buffers = (zero_half, zero_half, zero_full, zero_full)

    def usable(video_lengths):
        return tile_ids * TILE < jnp.repeat(video_lengths, per_video)

    group_count = lax.axis_size("grp")
    partner_bit = group_count.bit_length() - 2
    half_groups = group_count // 2
    partner_q, partner_k, partner_v, partner_g = partner(
        (own_data[0], own_data[1], own_data[2], own_data[3]), "grp", partner_bit
    )
    partner_data = (partner_q, partner_k, partner_v, partner_g)
    side = group // half_groups % 2
    other_group = jnp.where(side == 0, group + half_groups, group - half_groups)
    other_lengths = lengths[other_group]
    lower_lengths = jnp.where(side == 0, own_lengths, other_lengths)
    upper_lengths = jnp.where(side == 0, other_lengths, own_lengths)
    usable_all = jnp.concatenate([usable(lower_lengths), usable(upper_lengths)])
    ranks = jnp.cumsum(usable_all.astype(jnp.int32)) - usable_all.astype(jnp.int32)
    mine_all = usable_all & (ranks % 2 == side)
    half_count = 2 * per_video
    own_mine = jnp.where(side == 0, mine_all[:half_count], mine_all[half_count:])
    other_mine = jnp.where(side == 0, mine_all[half_count:], mine_all[:half_count])
    own_buffers = run_tasks(own_data, own_lengths, own_mine, start_buffers)
    other_buffers = run_tasks(partner_data, other_lengths, other_mine, start_buffers)
    back_out, back_qgrad, back_key, back_value = send_back(other_buffers, partner_bit)
    output = own_buffers[0] + back_out
    query_grad = own_buffers[1] + back_qgrad
    key_acc = own_buffers[2] + back_key
    value_acc = own_buffers[3] + back_value
    key_half = key_acc.astype(jnp.bfloat16)
    value_half = value_acc.astype(jnp.bfloat16)
    shaped = tuple(
        (
            item.reshape(1, 2, MAX_LEN, local_heads, HD)
            for item in (output, query_grad, key_half, value_half)
        )
    )
    out_tok, qgrad_tok, kgrad_tok, vgrad_tok = sent_together(
        (shaped[0], shaped[1], shaped[2], shaped[3]), "seq", 2, 3, 0
    )
    width = HEADS * HD
    return (
        out_tok.reshape(1, 2, local_rows, width),
        qgrad_tok.reshape(1, 2, local_rows, width),
        kgrad_tok.reshape(1, 2, local_rows, width),
        vgrad_tok.reshape(1, 2, local_rows, width),
    )


def solution(mesh):
    return jax.shard_map(
        per_device,
        mesh=mesh,
        in_specs=(
            P("grp", None, "seq", None),
            P("grp", None, "seq", None),
            P("grp", None, "seq", None),
            P("grp", None, "seq", None),
            P(),
        ),
        out_specs=(
            P("grp", None, "seq", None),
            P("grp", None, "seq", None),
            P("grp", None, "seq", None),
            P("grp", None, "seq", None),
        ),
        check_vma=False,
    )
```

profile of v0, /device:TPU:32, one launch (start us, length us, event | category | flops | bytes accessed | tf_op | source)
XLA Modules:
  0.0 874.2 jit_solution(2215363272256581158)
XLA Ops:
  3.2 11.4 %all-to-all-start = ((bf16[1,2,80,32,128]{4,2,1,0,3:T(8,128)(2,1)}), bf16[1,2,80,32,128]{4,2,1,0,3:T(8,128)(2,1)S(1)}, u32[]{:S(2)}, u32[]{:S(2)}) async-start(bf16[1,2,80,32,128]{4,2,1,0,3:T(8,128)(2,1)} %copy_bitcast_fusion.3), calls=%async_computation | async-start | bytes 2621440 | tf_op jit(solution)/shard_map/all_to_all | solution.py:134
  15.9 32.6 %all-to-all-done = bf16[1,2,80,32,128]{4,2,1,0,3:T(8,128)(2,1)S(1)} async-done(((bf16[1,2,80,32,128]{4,2,1,0,3:T(8,128)(2,1)}), bf16[1,2,80,32,128]{4,2,1,0,3:T(8,128)(2,1)S(1)}, u32[]{:S(2)}, u32[]{:S(2)}) %all-to-all-start) | async-done | bytes 1310752 | tf_op jit(solution)/shard_map/all_to_all | solution.py:134
  48.5 5.4 all-to-all-start.1
  56.5 30.8 %all-to-all-done.1 = bf16[1,2,80,32,128]{4,2,1,0,3:T(8,128)(2,1)S(1)} async-done(((bf16[1,2,80,32,128]{4,2,1,0,3:T(8,128)(2,1)}), bf16[1,2,80,32,128]{4,2,1,0,3:T(8,128)(2,1)S(1)}, u32[]{:S(2)}, u32[]{:S(2)}) %all-to-all-start.1) | async-done | bytes 1310752 | tf_op jit(solution)/shard_map/all_to_all | solution.py:132
  87.4 5.5 all-to-all-start.3
  95.5 30.8 %all-to-all-done.3 = bf16[1,2,80,32,128]{4,2,1,0,3:T(8,128)(2,1)} async-done(((bf16[1,2,80,32,128]{4,2,1,0,3:T(8,128)(2,1)}), bf16[1,2,80,32,128]{4,2,1,0,3:T(8,128)(2,1)}, u32[]{:S(2)}, u32[]{:S(2)}) %all-to-all-start.3) | async-done | bytes 1310752 | tf_op jit(solution)/shard_map/all_to_all | solution.py:135
  126.3 5.5 all-to-all-start.2
  142.2 23.1 %all-to-all-done.2 = bf16[1,2,80,32,128]{4,2,1,0,3:T(8,128)(2,1)} async-done(((bf16[1,2,80,32,128]{4,2,1,0,3:T(8,128)(2,1)}), bf16[1,2,80,32,128]{4,2,1,0,3:T(8,128)(2,1)}, u32[]{:S(2)}, u32[]{:S(2)}) %all-to-all-start.2) | async-done | bytes 1310752 | tf_op jit(solution)/shard_map/all_to_all | solution.py:133
  171.9 50.7 %collective-permute-done.3 = bf16[5120,1,128]{2,0,1:T(8,128)(2,1)} collective-permute-done((bf16[5120,1,128]{2,0,1:T(8,128)(2,1)}, bf16[5120,1,128]{2,0,1:T(8,128)(2,1)}, u32[]{:S(2)}, u32[]{:S(2)}) %collective-permute-start.3) | collective-permute-done | bytes 1310752 | tf_op jit(solution)/shard_map/ppermute | solution.py:15
  225.1 23.4 %collective-permute-done.2 = bf16[5120,1,128]{2,0,1:T(8,128)(2,1)} collective-permute-done((bf16[5120,1,128]{2,0,1:T(8,128)(2,1)S(1)}, bf16[5120,1,128]{2,0,1:T(8,128)(2,1)}, u32[]{:S(2)}, u32[]{:S(2)}) %collective-permute-start.2) | collective-permute-done | bytes 1310752 | tf_op jit(solution)/shard_map/ppermute | solution.py:15
  254.5 110.9 %while.49 = (s32[]{:T(128)}, bf16[5120,1,128]{0,2,1:T(8,128)(2,1)}, bf16[5120,1,128]{0,2,1:T(8,128)(2,1)}, f32[5120,1,128]{0,2,1:T(8,128)}, f32[5120,1,128]{0,2,...) while((s32[]{:T(128)}, bf16[5120,1,128]{0,2,1:T(8,128)(2,1)}, ...), condition=%wide.region_48.49_spmd, body=%wide.region_25.48_spmd.sunk | while | flops 2031749120 | bytes 111563808 | solution.py:116
  284.7 36.1 %conditional.9 = ((bf16[5120,1,128]{0,2,1:T(8,128)(2,1)}, bf16[5120,1,128]{0,2,1:T(8,128)(2,1)}, f32[5120,1,128]{0,2,1:T(8,128)}, f32[5120,1,128]{0,2,1:T(8,128)})) conditional(s32[]{:T(128)} %bitcast.557, (bf16[5120,1,128]{0,2,1:T(8,128)(2,1)}, bf16[5120,1,128]{0,2,1:T(8,128)(2,1)}, f32[5120,1,128]{0,2,1:T(8,128)}, ...), branch_computations={%region_26.26_spmd, %region_27.47_spmd.clone} | conditional | flops 2031749120 | bytes 111563376 | solution.py:114
  285.4 35.5 %conditional.5 = (bf16[5120,1,128]{0,2,1:T(8,128)(2,1)}, bf16[5120,1,128]{0,2,1:T(8,128)(2,1)}, f32[5120,1,128]{0,2,1:T(8,128)}, f32[5120,1,128]{0,2,1:T(8,128)}) conditional(s32[]{:T(128)} %clamp.13, (s32[]{:T(128)}, bf16[5120,1,128]{2,0,1:T(8,128)(2,1)}, s32[]{:T(128)}, s32[]{:T(128)}, s32[]{:T(128)}, ...), branch_computations={%region_28.30_spmd, %region_32.34_spmd, %region_36.38_spmd, %regio... | conditional | flops 2031749120 | bytes 111563008 | solution.py:109
  297.8 3.5 multiply_convert_fusion.4
  306.8 5.5 dynamic_update_slice.114
  315.4 5.5 dynamic_update_slice.115
  324.9 36.2 %conditional.9 = ((bf16[5120,1,128]{0,2,1:T(8,128)(2,1)}, bf16[5120,1,128]{0,2,1:T(8,128)(2,1)}, f32[5120,1,128]{0,2,1:T(8,128)}, f32[5120,1,128]{0,2,1:T(8,128)})) conditional(s32[]{:T(128)} %bitcast.557, (bf16[5120,1,128]{0,2,1:T(8,128)(2,1)}, bf16[5120,1,128]{0,2,1:T(8,128)(2,1)}, f32[5120,1,128]{0,2,1:T(8,128)}, ...), branch_computations={%region_26.26_spmd, %region_27.47_spmd.clone} | conditional | flops 2031749120 | bytes 111563376 | solution.py:114
  325.5 35.5 %conditional.5 = (bf16[5120,1,128]{0,2,1:T(8,128)(2,1)}, bf16[5120,1,128]{0,2,1:T(8,128)(2,1)}, f32[5120,1,128]{0,2,1:T(8,128)}, f32[5120,1,128]{0,2,1:T(8,128)}) conditional(s32[]{:T(128)} %clamp.13, (s32[]{:T(128)}, bf16[5120,1,128]{2,0,1:T(8,128)(2,1)}, s32[]{:T(128)}, s32[]{:T(128)}, s32[]{:T(128)}, ...), branch_computations={%region_28.30_spmd, %region_32.34_spmd, %region_36.38_spmd, %regio... | conditional | flops 2031749120 | bytes 111563008 | solution.py:109
  337.9 3.5 multiply_convert_fusion.4
  346.9 5.5 dynamic_update_slice.114
  355.5 5.5 dynamic_update_slice.115
  365.4 3.2 copy.79
  368.6 87.2 %collective-permute-start.7 = (f32[5120,1,128]{2,0,1:T(8,128)}, f32[5120,1,128]{2,0,1:T(8,128)}, u32[]{:S(2)}, u32[]{:S(2)}) collective-permute-start(f32[5120,1,128]{2,0,1:T(8,128)} %copy.79), channel_id=1, source_target_pairs={{0,128},{32,160},{64,192},{96,224},{128,0},{160,32},{192,64},{224,... | collective-permute-start | bytes 7864328 | tf_op jit(solution)/shard_map/ppermute | solution.py:15
  455.8 3.2 copy.77
  461.5 3.5 collective-permute-start.5
  475.8 215.8 %while.48 = (s32[]{:T(128)}, bf16[5120,1,128]{0,2,1:T(8,128)(2,1)}, bf16[5120,1,128]{0,2,1:T(8,128)(2,1)}, f32[5120,1,128]{0,2,1:T(8,128)}, f32[5120,1,128]{0,2,...) while((s32[]{:T(128)}, bf16[5120,1,128]{0,2,1:T(8,128)(2,1)}, ...), condition=%wide.region_24.25_spmd, body=%wide.region_1.24_spmd.sunk | while | flops 2031749120 | bytes 111564320 | solution.py:116
  478.0 41.0 %conditional.8 = ((bf16[5120,1,128]{0,2,1:T(8,128)(2,1)}, bf16[5120,1,128]{0,2,1:T(8,128)(2,1)}, f32[5120,1,128]{0,2,1:T(8,128)}, f32[5120,1,128]{0,2,1:T(8,128)})) conditional(s32[]{:T(128)} %bitcast.555, (bf16[5120,1,128]{0,2,1:T(8,128)(2,1)}, bf16[5120,1,128]{0,2,1:T(8,128)(2,1)}, f32[5120,1,128]{0,2,1:T(8,128)}, ...), branch_computations={%region_2.2_spmd, %region_3.23_spmd.clone} | conditional | flops 2031749120 | bytes 111563888 | solution.py:114
  478.7 40.2 %conditional.4 = (bf16[5120,1,128]{0,2,1:T(8,128)(2,1)}, bf16[5120,1,128]{0,2,1:T(8,128)(2,1)}, f32[5120,1,128]{0,2,1:T(8,128)}, f32[5120,1,128]{0,2,1:T(8,128)}) conditional(s32[]{:T(128)} %clamp.12, (s32[]{:T(128)}, bf16[5120,1,128]{2,0,1:T(8,128)(2,1)}, s32[]{:T(128)}, s32[]{:T(128)}, s32[]{:T(128)}, ...), branch_computations={%region_4.6_spmd, %region_8.10_spmd, %region_12.14_spmd, %region_1... | conditional | flops 2031749120 | bytes 111563520 | solution.py:109
  484.4 3.1 divide_select_fusion.6
  492.1 4.0 multiply_convert_fusion.2
  503.3 6.0 dynamic_update_slice.98
  509.3 3.6 fusion.136
  512.9 6.1 dynamic_update_slice.99
  522.9 41.0 %conditional.8 = ((bf16[5120,1,128]{0,2,1:T(8,128)(2,1)}, bf16[5120,1,128]{0,2,1:T(8,128)(2,1)}, f32[5120,1,128]{0,2,1:T(8,128)}, f32[5120,1,128]{0,2,1:T(8,128)})) conditional(s32[]{:T(128)} %bitcast.555, (bf16[5120,1,128]{0,2,1:T(8,128)(2,1)}, bf16[5120,1,128]{0,2,1:T(8,128)(2,1)}, f32[5120,1,128]{0,2,1:T(8,128)}, ...), branch_computations={%region_2.2_spmd, %region_3.23_spmd.clone} | conditional | flops 2031749120 | bytes 111563888 | solution.py:114
  523.7 40.2 %conditional.4 = (bf16[5120,1,128]{0,2,1:T(8,128)(2,1)}, bf16[5120,1,128]{0,2,1:T(8,128)(2,1)}, f32[5120,1,128]{0,2,1:T(8,128)}, f32[5120,1,128]{0,2,1:T(8,128)}) conditional(s32[]{:T(128)} %clamp.12, (s32[]{:T(128)}, bf16[5120,1,128]{2,0,1:T(8,128)(2,1)}, s32[]{:T(128)}, s32[]{:T(128)}, s32[]{:T(128)}, ...), branch_computations={%region_4.6_spmd, %region_8.10_spmd, %region_12.14_spmd, %region_1... | conditional | flops 2031749120 | bytes 111563520 | solution.py:109
  529.4 3.1 divide_select_fusion.6
  537.1 4.0 multiply_convert_fusion.2
  548.2 6.0 dynamic_update_slice.98
  554.3 3.6 fusion.136
  557.8 6.1 dynamic_update_slice.99
  567.9 41.0 %conditional.8 = ((bf16[5120,1,128]{0,2,1:T(8,128)(2,1)}, bf16[5120,1,128]{0,2,1:T(8,128)(2,1)}, f32[5120,1,128]{0,2,1:T(8,128)}, f32[5120,1,128]{0,2,1:T(8,128)})) conditional(s32[]{:T(128)} %bitcast.555, (bf16[5120,1,128]{0,2,1:T(8,128)(2,1)}, bf16[5120,1,128]{0,2,1:T(8,128)(2,1)}, f32[5120,1,128]{0,2,1:T(8,128)}, ...), branch_computations={%region_2.2_spmd, %region_3.23_spmd.clone} | conditional | flops 2031749120 | bytes 111563888 | solution.py:114
  568.6 40.2 %conditional.4 = (bf16[5120,1,128]{0,2,1:T(8,128)(2,1)}, bf16[5120,1,128]{0,2,1:T(8,128)(2,1)}, f32[5120,1,128]{0,2,1:T(8,128)}, f32[5120,1,128]{0,2,1:T(8,128)}) conditional(s32[]{:T(128)} %clamp.12, (s32[]{:T(128)}, bf16[5120,1,128]{2,0,1:T(8,128)(2,1)}, s32[]{:T(128)}, s32[]{:T(128)}, s32[]{:T(128)}, ...), branch_computations={%region_4.6_spmd, %region_8.10_spmd, %region_12.14_spmd, %region_1... | conditional | flops 2031749120 | bytes 111563520 | solution.py:109
  582.1 4.0 multiply_convert_fusion.2
  593.2 6.0 dynamic_update_slice.98
  599.3 3.6 fusion.136
  602.8 6.1 dynamic_update_slice.99
  612.9 36.2 %conditional.8 = ((bf16[5120,1,128]{0,2,1:T(8,128)(2,1)}, bf16[5120,1,128]{0,2,1:T(8,128)(2,1)}, f32[5120,1,128]{0,2,1:T(8,128)}, f32[5120,1,128]{0,2,1:T(8,128)})) conditional(s32[]{:T(128)} %bitcast.555, (bf16[5120,1,128]{0,2,1:T(8,128)(2,1)}, bf16[5120,1,128]{0,2,1:T(8,128)(2,1)}, f32[5120,1,128]{0,2,1:T(8,128)}, ...), branch_computations={%region_2.2_spmd, %region_3.23_spmd.clone} | conditional | flops 2031749120 | bytes 111563888 | solution.py:114
  613.6 35.5 %conditional.4 = (bf16[5120,1,128]{0,2,1:T(8,128)(2,1)}, bf16[5120,1,128]{0,2,1:T(8,128)(2,1)}, f32[5120,1,128]{0,2,1:T(8,128)}, f32[5120,1,128]{0,2,1:T(8,128)}) conditional(s32[]{:T(128)} %clamp.12, (s32[]{:T(128)}, bf16[5120,1,128]{2,0,1:T(8,128)(2,1)}, s32[]{:T(128)}, s32[]{:T(128)}, s32[]{:T(128)}, ...), branch_computations={%region_4.6_spmd, %region_8.10_spmd, %region_12.14_spmd, %region_1... | conditional | flops 2031749120 | bytes 111563520 | solution.py:109
  625.9 3.5 multiply_convert_fusion.1
  634.8 5.7 dynamic_update_slice.94
  643.6 5.5 dynamic_update_slice.95
  653.1 36.2 %conditional.8 = ((bf16[5120,1,128]{0,2,1:T(8,128)(2,1)}, bf16[5120,1,128]{0,2,1:T(8,128)(2,1)}, f32[5120,1,128]{0,2,1:T(8,128)}, f32[5120,1,128]{0,2,1:T(8,128)})) conditional(s32[]{:T(128)} %bitcast.555, (bf16[5120,1,128]{0,2,1:T(8,128)(2,1)}, bf16[5120,1,128]{0,2,1:T(8,128)(2,1)}, f32[5120,1,128]{0,2,1:T(8,128)}, ...), branch_computations={%region_2.2_spmd, %region_3.23_spmd.clone} | conditional | flops 2031749120 | bytes 111563888 | solution.py:114
  653.9 35.5 %conditional.4 = (bf16[5120,1,128]{0,2,1:T(8,128)(2,1)}, bf16[5120,1,128]{0,2,1:T(8,128)(2,1)}, f32[5120,1,128]{0,2,1:T(8,128)}, f32[5120,1,128]{0,2,1:T(8,128)}) conditional(s32[]{:T(128)} %clamp.12, (s32[]{:T(128)}, bf16[5120,1,128]{2,0,1:T(8,128)(2,1)}, s32[]{:T(128)}, s32[]{:T(128)}, s32[]{:T(128)}, ...), branch_computations={%region_4.6_spmd, %region_8.10_spmd, %region_12.14_spmd, %region_1... | conditional | flops 2031749120 | bytes 111563520 | solution.py:109
  666.1 3.5 multiply_convert_fusion.1
  675.1 5.7 dynamic_update_slice.94
  683.9 5.5 dynamic_update_slice.95
  691.6 3.3 copy.80
  694.8 3.2 copy.78
  711.7 20.6 %copy.81 = bf16[4,2,2560,1,128]{4,1,0,3,2:T(2,128)(2,1)S(1)} copy(bf16[4,2,2560,1,128]{4,2,1,3,0:T(8,128)(2,1)S(1)} %pad_maximum_fusion) | data formatting | bytes 10485760 | tf_op jit(solution)/shard_map/concatenate | solution.py:23
  732.3 119.0 %all_to_all.75 = bf16[4,2,2560,1,128]{4,1,0,3,2:T(2,128)(2,1)S(1)} all-to-all(bf16[4,2,2560,1,128]{4,1,0,3,2:T(2,128)(2,1)S(1)} %copy.81), channel_id=1, replica_groups=mesh['grp'=8,'seq'=32] {'seq'}, dimensions={2} | all-to-all | bytes 10485760 | tf_op jit(solution)/shard_map/all_to_all | solution.py:26
  855.3 3.2 reshape.888
  861.3 3.2 reshape.889
  865.9 3.2 reshape.890
  870.6 3.2 reshape.891
  (245 shorter events, 234.4 us)
Async XLA Ops:
  0.6 1.3 copy-start
  0.6 14.0 %copy-start.26 = (bf16[1,2,80,4096]{3,2,1,0:T(8,128)(2,1)S(1)}, bf16[1,2,80,4096]{3,2,1,0:T(8,128)(2,1)}, u32[]{:S(2)}) copy-start(bf16[1,2,80,4096]{3,2,1,0:T(8,128)(2,1)} %param.23) | copy-start | bytes 3932164
  3.2 45.3 %all-to-all-start = ((bf16[1,2,80,32,128]{4,2,1,0,3:T(8,128)(2,1)}), bf16[1,2,80,32,128]{4,2,1,0,3:T(8,128)(2,1)S(1)}, u32[]{:S(2)}, u32[]{:S(2)}) async-start(bf16[1,2,80,32,128]{4,2,1,0,3:T(8,128)(2,1)} %copy_bitcast_fusion.3), calls=%async_computation | async-start | bytes 2621440 | tf_op jit(solution)/shard_map/all_to_all | solution.py:134
  48.5 38.8 %all-to-all-start.1 = ((bf16[1,2,80,32,128]{4,2,1,0,3:T(8,128)(2,1)}), bf16[1,2,80,32,128]{4,2,1,0,3:T(8,128)(2,1)S(1)}, u32[]{:S(2)}, u32[]{:S(2)}) async-start(bf16[1,2,80,32,128]{4,2,1,0,3:T(8,128)(2,1)} %copy_bitcast_fusion.2), calls=%async_computation.1 | async-start | bytes 2621440 | tf_op jit(solution)/shard_map/all_to_all | solution.py:132
  87.3 8.1 copy-start.24
  87.4 38.9 %all-to-all-start.3 = ((bf16[1,2,80,32,128]{4,2,1,0,3:T(8,128)(2,1)}), bf16[1,2,80,32,128]{4,2,1,0,3:T(8,128)(2,1)}, u32[]{:S(2)}, u32[]{:S(2)}) async-start(bf16[1,2,80,32,128]{4,2,1,0,3:T(8,128)(2,1)} %copy_bitcast_fusion), calls=%async_computation.3 | async-start | bytes 2621440 | tf_op jit(solution)/shard_map/all_to_all | solution.py:135
  126.3 38.9 %all-to-all-start.2 = ((bf16[1,2,80,32,128]{4,2,1,0,3:T(8,128)(2,1)}), bf16[1,2,80,32,128]{4,2,1,0,3:T(8,128)(2,1)}, u32[]{:S(2)}, u32[]{:S(2)}) async-start(bf16[1,2,80,32,128]{4,2,1,0,3:T(8,128)(2,1)} %copy_bitcast_fusion.1), calls=%async_computation.2 | async-start | bytes 2621440 | tf_op jit(solution)/shard_map/all_to_all | solution.py:133
  131.8 4.2 copy-start.25
  133.0 92.1 %collective-permute-start = (bf16[5120,1,128]{2,0,1:T(8,128)(2,1)}, bf16[5120,1,128]{2,0,1:T(8,128)(2,1)}, u32[]{:S(2)}, u32[]{:S(2)}) collective-permute-start(bf16[5120,1,128]{2,0,1:T(8,128)(2,1)} %bitcast.138), channel_id=1, source_target_pairs={{0,128},{32,160},{64,192},{96,224},{128,0},{160,32},{192,64},{224,... | collective-permute-start | bytes 3932168 | tf_op jit(solution)/shard_map/ppermute | solution.py:15
  136.1 30.6 %copy-start.21 = (bf16[1,2,80,32,128]{4,2,3,1,0:T(8,128)(2,1)}, bf16[1,2,80,32,128]{4,2,3,1,0:T(8,128)(2,1)S(1)}, u32[]{:S(2)}) copy-start(bf16[1,2,80,32,128]{4,2,3,1,0:T(8,128)(2,1)S(1)} %copy.66) | copy-start | bytes 3932164
  136.1 33.7 %copy-start.27 = (s32[8,2]{0,1:T(2,128)S(1)}, s32[8,2]{0,1:T(2,128)}, u32[]{:S(2)}) copy-start(s32[8,2]{0,1:T(2,128)} %param.27) | copy-start | bytes 196
  136.1 89.0 %collective-permute-start.1 = (bf16[5120,1,128]{2,0,1:T(8,128)(2,1)S(1)}, bf16[5120,1,128]{2,0,1:T(8,128)(2,1)}, u32[]{:S(2)}, u32[]{:S(2)}) collective-permute-start(bf16[5120,1,128]{2,0,1:T(8,128)(2,1)S(1)} %bitcast.561), channel_id=1, source_target_pairs={{0,128},{32,160},{64,192},{96,224},{128,0},{160,32},{192,64},{224,... | collective-permute-start | bytes 3932168 | tf_op jit(solution)/shard_map/ppermute | solution.py:15
  139.3 83.3 %collective-permute-start.3 = (bf16[5120,1,128]{2,0,1:T(8,128)(2,1)}, bf16[5120,1,128]{2,0,1:T(8,128)(2,1)}, u32[]{:S(2)}, u32[]{:S(2)}) collective-permute-start(bf16[5120,1,128]{2,0,1:T(8,128)(2,1)} %bitcast.147), channel_id=1, source_target_pairs={{0,128},{32,160},{64,192},{96,224},{128,0},{160,32},{192,64},{224,... | collective-permute-start | bytes 3932168 | tf_op jit(solution)/shard_map/ppermute | solution.py:15
  166.6 84.3 %copy-start.18 = (bf16[1,2,80,32,128]{4,2,3,1,0:T(8,128)(2,1)}, bf16[1,2,80,32,128]{4,2,3,1,0:T(8,128)(2,1)S(1)}, u32[]{:S(2)}) copy-start(bf16[1,2,80,32,128]{4,2,3,1,0:T(8,128)(2,1)S(1)} %copy.68) | copy-start | bytes 3932164
  166.7 81.8 %collective-permute-start.2 = (bf16[5120,1,128]{2,0,1:T(8,128)(2,1)S(1)}, bf16[5120,1,128]{2,0,1:T(8,128)(2,1)}, u32[]{:S(2)}, u32[]{:S(2)}) collective-permute-start(bf16[5120,1,128]{2,0,1:T(8,128)(2,1)S(1)} %bitcast.559), channel_id=1, source_target_pairs={{0,128},{32,160},{64,192},{96,224},{128,0},{160,32},{192,64},{224,... | collective-permute-start | bytes 3932168 | tf_op jit(solution)/shard_map/ppermute | solution.py:15
  170.0 0.6 copy-start.28
  288.1 1.9 copy-start.10
  293.6 2.5 copy-start.4
  328.2 1.9 copy-start.10
  333.7 2.5 copy-start.4
  368.6 337.6 %collective-permute-start.7 = (f32[5120,1,128]{2,0,1:T(8,128)}, f32[5120,1,128]{2,0,1:T(8,128)}, u32[]{:S(2)}, u32[]{:S(2)}) collective-permute-start(f32[5120,1,128]{2,0,1:T(8,128)} %copy.79), channel_id=1, source_target_pairs={{0,128},{32,160},{64,192},{96,224},{128,0},{160,32},{192,64},{224,... | collective-permute-start | bytes 7864328 | tf_op jit(solution)/shard_map/ppermute | solution.py:15
  459.1 249.5 %collective-permute-start.6 = (f32[5120,1,128]{2,0,1:T(8,128)}, f32[5120,1,128]{2,0,1:T(8,128)}, u32[]{:S(2)}, u32[]{:S(2)}) collective-permute-start(f32[5120,1,128]{2,0,1:T(8,128)} %copy.77), channel_id=1, source_target_pairs={{0,128},{32,160},{64,192},{96,224},{128,0},{160,32},{192,64},{224,... | collective-permute-start | bytes 7864328 | tf_op jit(solution)/shard_map/ppermute | solution.py:15
  461.5 240.8 %collective-permute-start.5 = (bf16[5120,1,128]{2,0,1:T(8,128)(2,1)}, bf16[5120,1,128]{2,0,1:T(8,128)(2,1)}, u32[]{:S(2)}, u32[]{:S(2)}) collective-permute-start(bf16[5120,1,128]{2,0,1:T(8,128)(2,1)} %copy.75), channel_id=1, source_target_pairs={{0,128},{32,160},{64,192},{96,224},{128,0},{160,32},{192,64},{224,... | collective-permute-start | bytes 3932168 | tf_op jit(solution)/shard_map/ppermute | solution.py:15
  467.4 236.9 %collective-permute-start.4 = (bf16[5120,1,128]{2,0,1:T(8,128)(2,1)}, bf16[5120,1,128]{2,0,1:T(8,128)(2,1)}, u32[]{:S(2)}, u32[]{:S(2)}) collective-permute-start(bf16[5120,1,128]{2,0,1:T(8,128)(2,1)} %copy.73), channel_id=1, source_target_pairs={{0,128},{32,160},{64,192},{96,224},{128,0},{160,32},{192,64},{224,... | collective-permute-start | bytes 3932168 | tf_op jit(solution)/shard_map/ppermute | solution.py:15
  472.3 3.5 copy-start.19
  472.3 3.5 copy-start.29
  472.3 3.5 copy-start.30
  481.4 2.3 copy-start.7
  487.6 2.8 copy-start.3
  496.2 1.5 copy-start.15
  526.4 2.3 copy-start.7
  532.5 2.8 copy-start.3
  541.1 1.5 copy-start.15
  571.4 2.3 copy-start.7
  577.5 2.8 copy-start.3
  586.1 1.5 copy-start.15
  616.1 1.9 copy-start.11
  621.6 2.5 copy-start.5
  656.4 1.9 copy-start.11
  661.9 2.5 copy-start.5
  704.3 2.1 copy-start.23
  706.2 2.6 copy-start.22
  869.1 4.6 copy-start.1
where the time goes:
time: 884 us; the launch traced here: 874 us
  local copies, waits for them, and re-layouts  241 us (27%)
  waiting for transfers between devices  191 us (22%)
  starting transfers between devices  128 us (14%)
  blocking collectives  119 us (13%)
  matrix products  107 us (12%)
  other arithmetic  46.5 us (5%)
  loops' own time  39.3 us (4%)
    all_to_all x1, blocking collectives, sent_together(): lax.all_to_all(both, axis, split_axis=split_dim, concat_axis=concat_dim,...  119 us
    ppermute x8, starting transfers between devices, partner(): return lax.ppermute(value, axis, pairs)  101 us
    ppermute x8, waiting for transfers between devices, partner(): return lax.ppermute(value, axis, pairs)  74.1 us
    dynamic_update_slice x7, local copies, waits for them, and re-layouts, compute(): lax.dynamic_update_slice_in_dim(key_acc, lax.dynamic_slice_in_dim(key_acc...  40.5 us
    dynamic_update_slice x7, local copies, waits for them, and re-layouts, compute(): lax.dynamic_update_slice_in_dim(value_acc, lax.dynamic_slice_in_dim(value...  40.1 us
    another operation x2, loops' own time, run_tasks(): return lax.fori_loop(0, 2 * per_video, one_task, buffers)  33.3 us
    all_to_all x1, waiting for transfers between devices, per_device(): lax.all_to_all(value_split, 'seq', split_axis=3, concat_axis=2, tiled=True)  32.6 us
    all_to_all x1, waiting for transfers between devices, per_device(): lax.all_to_all(grad_split, 'seq', split_axis=3, concat_axis=2, tiled=True)  30.8 us
  transfers between devices with their start and end apart: 12, of which 6 were waited for; matrix products, arithmetic and copies ran while one was open for 28% of the time, Pallas kernels for 0%

commit v1 on v0

v1 whole, which is shorter than its diff:
```python
import jax
import jax.numpy as jnp
from jax import lax
from jax.experimental import pallas as pl
from jax.experimental.pallas import tpu as pltpu
from jax.sharding import PartitionSpec as P

HEADS = 32
HD = 128
MAX_LEN = 2560
SHARDS = 32
ROWS = MAX_LEN // SHARDS
TQ = 256
TK = 512
COLS = 8
LOG2E = 1.4426950408889634
SCALE = HD ** (-0.5)


def pack_body(q_ref, k_ref, v_ref, g_ref, out_ref):
    for number, ref in enumerate((q_ref, k_ref, v_ref, g_ref)):
        for h in range(COLS):
            out_ref[h, number] = ref[0, 0, :, h * HD : (h + 1) * HD]


def pack(arrays, video):
    spec = pl.BlockSpec((1, 1, ROWS, COLS * HD), lambda j: (0, video, 0, j))
    return pl.pallas_call(
        pack_body,
        grid=(HEADS // COLS,),
        in_specs=[spec] * 4,
        out_specs=pl.BlockSpec((COLS, 4, ROWS, HD), lambda j: (j, 0, 0, 0)),
        out_shape=jax.ShapeDtypeStruct((HEADS, 4, ROWS, HD), jnp.bfloat16),
        cost_estimate=pl.CostEstimate(flops=0, transcendentals=0, bytes_accessed=5242880),
        name=f"pack{video}",
    )(*arrays)


def unpack_body(in_ref, *refs):
    for number, ref in enumerate(refs[-4:]):
        for h in range(COLS):
            ref[0, 0, :, h * HD : (h + 1) * HD] = in_ref[h, number]


def unpack(back, video, earlier):
    spec = pl.BlockSpec((1, 1, ROWS, COLS * HD), lambda j: (0, video, 0, j))
    extra = [pl.BlockSpec(memory_space=pl.ANY)] * len(earlier)
    return pl.pallas_call(
        unpack_body,
        grid=(HEADS // COLS,),
        in_specs=[pl.BlockSpec((COLS, 4, ROWS, HD), lambda j: (j, 0, 0, 0))] + extra,
        out_specs=[spec] * 4,
        out_shape=[jax.ShapeDtypeStruct((1, 2, ROWS, HEADS * HD), jnp.bfloat16)] * 4,
        input_output_aliases={1 + i: i for i in range(len(earlier))},
        cost_estimate=pl.CostEstimate(flops=0, transcendentals=0, bytes_accessed=5242880),
        name=f"unpack{video}",
    )(back, *earlier)


def dot(a, b, dims):
    return lax.dot_general(a, b, (dims, ((), ())), preferred_element_type=jnp.float32)


def attend_body(
    len_ref, x_ref, out_ref, q_s, k_s, v_s, g_s, o_s, dq_s, s_s, w_s, dk_s, dv_s, m_s, l_s, acc_s
):
    length = len_ref[0]
    for s in range(SHARDS):
        rows = slice(s * ROWS, (s + 1) * ROWS)
        q_s[rows] = x_ref[s, 0]
        k_s[rows] = x_ref[s, 1]
        v_s[rows] = x_ref[s, 2]
        valid = lax.broadcasted_iota(jnp.int32, (ROWS, HD), 0) < length - s * ROWS
        g_s[rows] = jnp.where(valid, x_ref[s, 3].astype(jnp.float32), 0.0).astype(jnp.bfloat16)
    o_s[...] = jnp.zeros_like(o_s)
    dq_s[...] = jnp.zeros_like(dq_s)
    dk_s[...] = jnp.zeros_like(dk_s)
    dv_s[...] = jnp.zeros_like(dv_s)
    query_tiles = (length + TQ - 1) // TQ
    key_tiles = (length + TK - 1) // TK
    fold = SCALE * LOG2E

    def query_tile(i, _):
        r0 = pl.multiple_of(i * TQ, TQ)
        m_s[...] = jnp.full_like(m_s, -3.0e38)
        l_s[...] = jnp.zeros_like(l_s)
        acc_s[...] = jnp.zeros_like(acc_s)

        def score_pass(j, _):
            k0 = pl.multiple_of(j * TK, TK)
            s = dot(q_s[pl.ds(r0, TQ)], k_s[pl.ds(k0, TK)], ((1,), (1,)))
            col = lax.broadcasted_iota(jnp.int32, (1, TK), 1) + k0
            s = jnp.where(col < length, s, -1e30)
            s_s[:, pl.ds(k0, TK)] = s
            top = m_s[...]
            for c in range(TK // HD):
                top = jnp.maximum(top, s[:, c * HD : (c + 1) * HD])
            m_s[...] = top
            return 0

        lax.fori_loop(0, key_tiles, score_pass, 0)
        shift = jnp.max(m_s[...], axis=1, keepdims=True) * fold

        def weight_pass(j, _):
            k0 = pl.multiple_of(j * TK, TK)
            w = jnp.exp2(s_s[:, pl.ds(k0, TK)] * fold - shift)
            total = l_s[...]
            for c in range(TK // HD):
                total = total + w[:, c * HD : (c + 1) * HD]
            l_s[...] = total
            w = w.astype(jnp.bfloat16)
            w_s[:, pl.ds(k0, TK)] = w
            acc_s[...] += dot(w, v_s[pl.ds(k0, TK)], ((1,), (0,)))
            return 0

        lax.fori_loop(0, key_tiles, weight_pass, 0)
        inverse = 1.0 / jnp.sum(l_s[...], axis=1, keepdims=True)
        row = lax.broadcasted_iota(jnp.int32, (TQ, 1), 0) + r0
        output = jnp.where(row < length, acc_s[...] * inverse, 0.0).astype(jnp.bfloat16)
        o_s[pl.ds(r0, TQ)] = output
        delta = jnp.sum(
            g_s[pl.ds(r0, TQ)].astype(jnp.float32) * output.astype(jnp.float32),
            axis=1,
            keepdims=True,
        )
        acc_s[...] = jnp.zeros_like(acc_s)

        def grad_pass(j, _):
            k0 = pl.multiple_of(j * TK, TK)
            q = q_s[pl.ds(r0, TQ)]
            g = g_s[pl.ds(r0, TQ)]
            p = w_s[:, pl.ds(k0, TK)].astype(jnp.float32) * inverse
            dp = dot(g, v_s[pl.ds(k0, TK)], ((1,), (1,)))
            ds = (p * (dp - delta)).astype(jnp.bfloat16)
            acc_s[...] += dot(ds, k_s[pl.ds(k0, TK)], ((1,), (0,)))
            dk_s[pl.ds(k0, TK)] += dot(ds, q, ((0,), (0,)))
            dv_s[pl.ds(k0, TK)] += dot(p.astype(jnp.bfloat16), g, ((0,), (0,)))
            return 0

        lax.fori_loop(0, key_tiles, grad_pass, 0)
        dq_s[pl.ds(r0, TQ)] = (acc_s[...] * SCALE).astype(jnp.bfloat16)
        return 0

    lax.fori_loop(0, query_tiles, query_tile, 0)
    for s in range(SHARDS):
        rows = slice(s * ROWS, (s + 1) * ROWS)
        out_ref[s, 0] = o_s[rows]
        out_ref[s, 1] = dq_s[rows]
        out_ref[s, 2] = (dk_s[rows] * SCALE).astype(jnp.bfloat16)
        out_ref[s, 3] = dv_s[rows].astype(jnp.bfloat16)


def attend(length, received, video):
    half = pltpu.VMEM((MAX_LEN, HD), jnp.bfloat16)
    full = pltpu.VMEM((MAX_LEN, HD), jnp.float32)
    tile = pltpu.VMEM((TQ, HD), jnp.float32)
    return pl.pallas_call(
        attend_body,
        in_specs=[
            pl.BlockSpec(memory_space=pltpu.SMEM),
            pl.BlockSpec(memory_space=pltpu.VMEM),
        ],
        out_specs=pl.BlockSpec(memory_space=pltpu.VMEM),
        out_shape=jax.ShapeDtypeStruct((SHARDS, 4, ROWS, HD), jnp.bfloat16),
        scratch_shapes=[half] * 6
        + [
            pltpu.VMEM((TQ, MAX_LEN), jnp.float32),
            pltpu.VMEM((TQ, MAX_LEN), jnp.bfloat16),
            full,
            full,
            tile,
            tile,
            tile,
        ],
        compiler_params=pltpu.CompilerParams(vmem_limit_bytes=32 * 1024 * 1024),
        cost_estimate=pl.CostEstimate(
            flops=10 * MAX_LEN * MAX_LEN * HD,
            transcendentals=MAX_LEN * MAX_LEN,
            bytes_accessed=5242880,
        ),
        name=f"attend{video}",
    )(length, received)


def exchange(value):
    return lax.all_to_all(value, "seq", split_axis=0, concat_axis=0, tiled=True)


def per_device(query_rows, key_rows, value_rows, out_grad, lengths):
    arrays = (query_rows, key_rows, value_rows, out_grad)
    own = lax.dynamic_index_in_dim(lengths, lax.axis_index("grp"), 0, keepdims=False)
    outputs = ()
    for video in range(2):
        received = exchange(pack(arrays, video))
        computed = attend(own[video : video + 1], received, video)
        outputs = unpack(exchange(computed), video, outputs)
    return tuple(outputs)


def solution(mesh):
    rows = P("grp", None, "seq", None)
    return jax.shard_map(
        per_device,
        mesh=mesh,
        in_specs=(rows, rows, rows, rows, P()),
        out_specs=(rows, rows, rows, rows),
        check_vma=False,
    )
```

time: 884 us -> 290 us (0.33)
  the two profiles are of different devices: /device:TPU:32 before, /device:TPU:1 now
where the time goes in v1:
time: 290 us; the launch traced here: 286 us
  waiting for transfers between devices  169 us (58%)
  Pallas kernels  74 us (26%)
  starting transfers between devices  33.8 us (12%)
  local copies, waits for them, and re-layouts  8.34 us (3%)
    all_to_all x4, waiting for transfers between devices, exchange(): return lax.all_to_all(value, 'seq', split_axis=0, concat_axis=0, tiled=True)  169 us
    pallas_call x2, Pallas kernels, attend(): pl.pallas_call(attend_body, in_specs=[pl.BlockSpec(memory_space=pltpu.SME...  57.3 us
    all_to_all x4, starting transfers between devices, exchange(): return lax.all_to_all(value, 'seq', split_axis=0, concat_axis=0, tiled=True)  33.8 us
    pallas_call x2, Pallas kernels, pack(): pl.pallas_call(pack_body, grid=(HEADS // COLS,), in_specs=[spec] * 4, out...  8.43 us
    pallas_call x2, Pallas kernels, unpack(): pl.pallas_call(unpack_body, grid=(HEADS // COLS,), in_specs=[pl.BlockSpec...  8.34 us
    unnamed x12, local copies, waits for them, and re-layouts  7.75 us
  transfers between devices with their start and end apart: 4, of which 4 were waited for; matrix products, arithmetic and copies ran while one was open for 0% of the time, Pallas kernels for 23%

profile of v1, /device:TPU:1, one launch (start us, length us, event | category | flops | bytes accessed | tf_op | source)
XLA Modules:
  0.0 285.7 jit_solution(4806440928863621096)
XLA Ops:
  0.6 0.0 copy-start
  0.6 4.2 %pack0.1 = bf16[32,4,80,128]{3,2,1,0:T(8,128)(2,1)} custom-call(bf16[1,2,80,4096]{3,2,1,0:T(8,128)(2,1)} %q_ref.3, bf16[1,2,80,4096]{3,2,1,0:T(8,128)(2,1)} %k_ref.3, bf16[1,2,80,4096]{3,2,1,0:T(8,128)(2,1)} %v_ref.3, bf16[1,2,80,4096]{3,2,1,0:T(8,128)(2,1)} %g_ref.3), custom_call_target="tpu_custom_call" | custom-call | bytes 5242880 | tf_op jit(solution)/shard_map/pack0/pallas_call | solution.py:28
  4.9 12.0 %all-to-all-start.2 = ((bf16[32,4,80,128]{3,2,1,0:T(8,128)(2,1)}), bf16[32,4,80,128]{3,2,1,0:T(8,128)(2,1)S(1)}, u32[]{:S(2)}, u32[]{:S(2)}) async-start(bf16[32,4,80,128]{3,2,1,0:T(8,128)(2,1)} %pack0.1), calls=%async_computation.2 | async-start | bytes 5242880 | tf_op jit(solution)/shard_map/all_to_all | solution.py:186
  16.9 4.2 %pack1.1 = bf16[32,4,80,128]{3,2,1,0:T(8,128)(2,1)} custom-call(bf16[1,2,80,4096]{3,2,1,0:T(8,128)(2,1)} %q_ref.3, bf16[1,2,80,4096]{3,2,1,0:T(8,128)(2,1)} %k_ref.3, bf16[1,2,80,4096]{3,2,1,0:T(8,128)(2,1)} %v_ref.3, bf16[1,2,80,4096]{3,2,1,0:T(8,128)(2,1)} %g_ref.3), custom_call_target="tpu_custom_call" | custom-call | bytes 5242880 | tf_op jit(solution)/shard_map/pack1/pallas_call | solution.py:28
  21.1 55.8 %all-to-all-done.2.x_ref = bf16[32,4,80,128]{3,2,1,0:T(8,128)(2,1)S(1)} async-done(((bf16[32,4,80,128]{3,2,1,0:T(8,128)(2,1)}), bf16[32,4,80,128]{3,2,1,0:T(8,128)(2,1)S(1)}, u32[]{:S(2)}, u32[]{:S(2)}) %all-to-all-start.2) | async-done | bytes 2621472 | tf_op jit(solution)/shard_map/all_to_all | solution.py:186
  76.9 0.0 copy-start.1
  76.9 1.5 copy-done.1
  78.5 7.4 %all-to-all-start = ((bf16[32,4,80,128]{3,2,1,0:T(8,128)(2,1)}), bf16[32,4,80,128]{3,2,1,0:T(8,128)(2,1)S(1)}, u32[]{:S(2)}, u32[]{:S(2)}) async-start(bf16[32,4,80,128]{3,2,1,0:T(8,128)(2,1)} %pack1.1), calls=%async_computation | async-start | bytes 5242880 | tf_op jit(solution)/shard_map/all_to_all | solution.py:186
  85.9 0.0 copy-done
  85.9 0.1 constant_dynamic-slice_fusion
  86.0 0.5 fusion
  86.5 0.0 copy-start.2
  86.5 1.7 copy-done.2
  88.2 38.2 %attend0.1 = bf16[32,4,80,128]{3,2,1,0:T(8,128)(2,1)S(1)} custom-call(s32[1]{0:T(128)} %bitcast.1.len_ref, bf16[32,4,80,128]{3,2,1,0:T(8,128)(2,1)S(1)} %copy-done.2), custom_call_target="tpu_custom_call" | custom-call | flops 8388608000 | bytes 5242880 | tf_op jit(solution)/shard_map/attend0/pallas_call | solution.py:157
  126.4 0.0 copy-start.4
  126.5 1.5 copy-done.4
  128.0 17.6 %all-to-all-done.x_ref = bf16[32,4,80,128]{3,2,1,0:T(8,128)(2,1)S(1)} async-done(((bf16[32,4,80,128]{3,2,1,0:T(8,128)(2,1)}), bf16[32,4,80,128]{3,2,1,0:T(8,128)(2,1)S(1)}, u32[]{:S(2)}, u32[]{:S(2)}) %all-to-all-start) | async-done | bytes 2621472 | tf_op jit(solution)/shard_map/all_to_all | solution.py:186
  145.6 7.5 %all-to-all-start.3 = ((bf16[32,4,80,128]{3,2,1,0:T(8,128)(2,1)}), bf16[32,4,80,128]{3,2,1,0:T(8,128)(2,1)}, u32[]{:S(2)}, u32[]{:S(2)}) async-start(bf16[32,4,80,128]{3,2,1,0:T(8,128)(2,1)} %copy-done.4), calls=%async_computation.3 | async-start | bytes 5242880 | tf_op jit(solution)/shard_map/all_to_all | solution.py:186
  153.2 19.1 %attend1.1 = bf16[32,4,80,128]{3,2,1,0:T(8,128)(2,1)S(1)} custom-call(s32[1]{0:T(128)} %bitcast.len_ref, bf16[32,4,80,128]{3,2,1,0:T(8,128)(2,1)S(1)} %all-to-all-done.x_ref), custom_call_target="tpu_custom_call" | custom-call | flops 8388608000 | bytes 5242880 | tf_op jit(solution)/shard_map/attend1/pallas_call | solution.py:157
  172.2 0.0 copy-start.3
  172.2 1.5 copy-done.3
  173.7 39.6 %all-to-all-done.3.in_ref = bf16[32,4,80,128]{3,2,1,0:T(8,128)(2,1)} async-done(((bf16[32,4,80,128]{3,2,1,0:T(8,128)(2,1)}), bf16[32,4,80,128]{3,2,1,0:T(8,128)(2,1)}, u32[]{:S(2)}, u32[]{:S(2)}) %all-to-all-start.3) | async-done | bytes 2621472 | tf_op jit(solution)/shard_map/all_to_all | solution.py:186
  213.3 6.8 %all-to-all-start.1 = ((bf16[32,4,80,128]{3,2,1,0:T(8,128)(2,1)}), bf16[32,4,80,128]{3,2,1,0:T(8,128)(2,1)S(1)}, u32[]{:S(2)}, u32[]{:S(2)}) async-start(bf16[32,4,80,128]{3,2,1,0:T(8,128)(2,1)} %copy-done.3), calls=%async_computation.1 | async-start | bytes 5242880 | tf_op jit(solution)/shard_map/all_to_all | solution.py:186
  220.1 4.2 %unpack0.1 = (bf16[1,2,80,4096]{3,2,1,0:T(8,128)(2,1)}, bf16[1,2,80,4096]{3,2,1,0:T(8,128)(2,1)}, bf16[1,2,80,4096]{3,2,1,0:T(8,128)(2,1)}, bf16[1,2,80,4096]{3,2,1,0:T(8,128)(2,1)}) custom-call(bf16[32,4,80,128]{3,2,1,0:T(8,128)(2,1)} %all-to-all-done.3.in_ref), custom_call_target="tpu_custom_call" | custom-call | bytes 5242880 | tf_op jit(solution)/shard_map/unpack0/pallas_call | solution.py:48
  224.3 55.8 %all-to-all-done.1.in_ref = bf16[32,4,80,128]{3,2,1,0:T(8,128)(2,1)S(1)} async-done(((bf16[32,4,80,128]{3,2,1,0:T(8,128)(2,1)}), bf16[32,4,80,128]{3,2,1,0:T(8,128)(2,1)S(1)}, u32[]{:S(2)}, u32[]{:S(2)}) %all-to-all-start.1) | async-done | bytes 2621472 | tf_op jit(solution)/shard_map/all_to_all | solution.py:186
  280.1 0.0 copy-start.5
  280.1 1.5 copy-done.5
  281.5 4.2 %unpack1.1 = (bf16[1,2,80,4096]{3,2,1,0:T(8,128)(2,1)}, bf16[1,2,80,4096]{3,2,1,0:T(8,128)(2,1)}, bf16[1,2,80,4096]{3,2,1,0:T(8,128)(2,1)}, bf16[1,2,80,4096]{3,2,1,0:T(8,128)(2,1)}) custom-call(bf16[32,4,80,128]{3,2,1,0:T(8,128)(2,1)} %copy-done.5, ...), custom_call_target="tpu_custom_call", output_to_operand_aliasing={{0}: (1, {}), {1}: (2, {}), {2}: (3, {}), {3}: (4, {})} | custom-call | bytes 5242880 | tf_op jit(solution)/shard_map/unpack1/pallas_call | solution.py:48
Async XLA Ops:
  0.6 85.3 %copy-start = (s32[8,2]{0,1:T(2,128)S(1)}, s32[8,2]{0,1:T(2,128)}, u32[]{:S(2)}) copy-start(s32[8,2]{0,1:T(2,128)} %param.9) | copy-start | bytes 196
  4.9 72.1 %all-to-all-start.2 = ((bf16[32,4,80,128]{3,2,1,0:T(8,128)(2,1)}), bf16[32,4,80,128]{3,2,1,0:T(8,128)(2,1)S(1)}, u32[]{:S(2)}, u32[]{:S(2)}) async-start(bf16[32,4,80,128]{3,2,1,0:T(8,128)(2,1)} %pack0.1), calls=%async_computation.2 | async-start | bytes 5242880 | tf_op jit(solution)/shard_map/all_to_all | solution.py:186
  76.9 1.5 copy-start.1
  78.5 67.1 %all-to-all-start = ((bf16[32,4,80,128]{3,2,1,0:T(8,128)(2,1)}), bf16[32,4,80,128]{3,2,1,0:T(8,128)(2,1)S(1)}, u32[]{:S(2)}, u32[]{:S(2)}) async-start(bf16[32,4,80,128]{3,2,1,0:T(8,128)(2,1)} %pack1.1), calls=%async_computation | async-start | bytes 5242880 | tf_op jit(solution)/shard_map/all_to_all | solution.py:186
  86.5 1.7 copy-start.2
  126.4 1.5 copy-start.4
  145.6 67.7 %all-to-all-start.3 = ((bf16[32,4,80,128]{3,2,1,0:T(8,128)(2,1)}), bf16[32,4,80,128]{3,2,1,0:T(8,128)(2,1)}, u32[]{:S(2)}, u32[]{:S(2)}) async-start(bf16[32,4,80,128]{3,2,1,0:T(8,128)(2,1)} %copy-done.4), calls=%async_computation.3 | async-start | bytes 5242880 | tf_op jit(solution)/shard_map/all_to_all | solution.py:186
  172.2 1.5 copy-start.3
  213.3 66.8 %all-to-all-start.1 = ((bf16[32,4,80,128]{3,2,1,0:T(8,128)(2,1)}), bf16[32,4,80,128]{3,2,1,0:T(8,128)(2,1)S(1)}, u32[]{:S(2)}, u32[]{:S(2)}) async-start(bf16[32,4,80,128]{3,2,1,0:T(8,128)(2,1)} %copy-done.3), calls=%async_computation.1 | async-start | bytes 5242880 | tf_op jit(solution)/shard_map/all_to_all | solution.py:186
  280.1 1.5 copy-start.5

commit v2 on v1

--- a/solution.py
+++ b/solution.py
@@ -10,30 +10,35 @@
 MAX_LEN = 2560
 SHARDS = 32
 ROWS = MAX_LEN // SHARDS
-TQ = 256
-TK = 512
-COLS = 8
+TQ = 512
+TK = 2560
+STAGGER = 25000
+COLS = 16
 LOG2E = 1.4426950408889634
 SCALE = HD ** (-0.5)
 
 
-def pack_body(q_ref, k_ref, v_ref, g_ref, out_ref):
+def pack_body(wait_ref, q_ref, k_ref, v_ref, g_ref, out_ref):
+    @pl.when(jnp.logical_and(pl.program_id(0) == 0, wait_ref[0] == 1))
+    def _():
+        pl.delay(STAGGER)
+
     for number, ref in enumerate((q_ref, k_ref, v_ref, g_ref)):
         for h in range(COLS):
             out_ref[h, number] = ref[0, 0, :, h * HD : (h + 1) * HD]
 
 
-def pack(arrays, video):
+def pack(late, arrays, video):
     spec = pl.BlockSpec((1, 1, ROWS, COLS * HD), lambda j: (0, video, 0, j))
     return pl.pallas_call(
         pack_body,
         grid=(HEADS // COLS,),
-        in_specs=[spec] * 4,
+        in_specs=[pl.BlockSpec(memory_space=pltpu.SMEM)] + [spec] * 4,
         out_specs=pl.BlockSpec((COLS, 4, ROWS, HD), lambda j: (j, 0, 0, 0)),
         out_shape=jax.ShapeDtypeStruct((HEADS, 4, ROWS, HD), jnp.bfloat16),
         cost_estimate=pl.CostEstimate(flops=0, transcendentals=0, bytes_accessed=5242880),
         name=f"pack{video}",
-    )(*arrays)
+    )(late, *arrays)
 
 
 def unpack_body(in_ref, *refs):
@@ -62,9 +67,13 @@
 
 
 def attend_body(
-    len_ref, x_ref, out_ref, q_s, k_s, v_s, g_s, o_s, dq_s, s_s, w_s, dk_s, dv_s, m_s, l_s, acc_s
+    len_ref, x_hbm, out_hbm, x_ref, q_s, k_s, v_s, g_s, o_s, dq_s, s_s, w_s, dk_s, dv_s, m_s, l_s,
+    acc_s, sem
 ):
     length = len_ref[0]
+    load = pltpu.make_async_copy(x_hbm, x_ref, sem)
+    load.start()
+    load.wait()
     for s in range(SHARDS):
         rows = slice(s * ROWS, (s + 1) * ROWS)
         q_s[rows] = x_ref[s, 0]
@@ -144,10 +153,13 @@
     lax.fori_loop(0, query_tiles, query_tile, 0)
     for s in range(SHARDS):
         rows = slice(s * ROWS, (s + 1) * ROWS)
-        out_ref[s, 0] = o_s[rows]
-        out_ref[s, 1] = dq_s[rows]
-        out_ref[s, 2] = (dk_s[rows] * SCALE).astype(jnp.bfloat16)
-        out_ref[s, 3] = dv_s[rows].astype(jnp.bfloat16)
+        x_ref[s, 0] = o_s[rows]
+        x_ref[s, 1] = dq_s[rows]
+        x_ref[s, 2] = (dk_s[rows] * SCALE).astype(jnp.bfloat16)
+        x_ref[s, 3] = dv_s[rows].astype(jnp.bfloat16)
+    store = pltpu.make_async_copy(x_ref, out_hbm, sem)
+    store.start()
+    store.wait()
 
 
 def attend(length, received, video):
@@ -158,11 +170,12 @@
         attend_body,
         in_specs=[
             pl.BlockSpec(memory_space=pltpu.SMEM),
-            pl.BlockSpec(memory_space=pltpu.VMEM),
+            pl.BlockSpec(memory_space=pltpu.HBM),
         ],
-        out_specs=pl.BlockSpec(memory_space=pltpu.VMEM),
+        out_specs=pl.BlockSpec(memory_space=pltpu.HBM),
         out_shape=jax.ShapeDtypeStruct((SHARDS, 4, ROWS, HD), jnp.bfloat16),
-        scratch_shapes=[half] * 6
+        scratch_shapes=[pltpu.VMEM((SHARDS, 4, ROWS, HD), jnp.bfloat16)]
+        + [half] * 6
         + [
             pltpu.VMEM((TQ, MAX_LEN), jnp.float32),
             pltpu.VMEM((TQ, MAX_LEN), jnp.bfloat16),
@@ -171,8 +184,8 @@
             tile,
             tile,
             tile,
+            pltpu.SemaphoreType.DMA,
         ],
-        compiler_params=pltpu.CompilerParams(vmem_limit_bytes=32 * 1024 * 1024),
         cost_estimate=pl.CostEstimate(
             flops=10 * MAX_LEN * MAX_LEN * HD,
             transcendentals=MAX_LEN * MAX_LEN,
@@ -188,10 +201,12 @@
 
 def per_device(query_rows, key_rows, value_rows, out_grad, lengths):
     arrays = (query_rows, key_rows, value_rows, out_grad)
-    own = lax.dynamic_index_in_dim(lengths, lax.axis_index("grp"), 0, keepdims=False)
+    group = lax.axis_index("grp")
+    own = lax.dynamic_index_in_dim(lengths, group, 0, keepdims=False)
+    late = (group % 2).reshape(1)
     outputs = ()
     for video in range(2):
-        received = exchange(pack(arrays, video))
+        received = exchange(pack(late * (1 - video), arrays, video))
         computed = attend(own[video : video + 1], received, video)
         outputs = unpack(exchange(computed), video, outputs)
     return tuple(outputs)

time: 290 us -> 251 us (0.87); the launches traced: 286 us -> 250 us
  waiting for transfers between devices: 169 us -> 111 us
  Pallas kernels: 74 us -> 88.6 us
  starting transfers between devices: 33.8 us -> 44.9 us
  local copies, waits for them, and re-layouts: 8.34 us -> 5.03 us
    all_to_all x4, waiting for transfers between devices: 169 us -> 111 us  [exchange(): return lax.all_to_all(value, 'seq', split_axis=0, concat_axis=0, tiled=True)]
    pallas_call x2, Pallas kernels: 8.43 us -> 31.1 us  [pack(): pl.pallas_call(pack_body, grid=(HEADS // COLS,), in_specs=[pl.BlockSpec(m...]
    all_to_all x4, starting transfers between devices: 33.8 us -> 44.9 us  [exchange(): return lax.all_to_all(value, 'seq', split_axis=0, concat_axis=0, tiled=True)]
    pallas_call x2, Pallas kernels: 57.3 us -> 51.4 us  [attend(): pl.pallas_call(attend_body, in_specs=[pl.BlockSpec(memory_space=pltpu.SME...]
    unnamed x12 -> x8, local copies, waits for them, and re-layouts: 7.75 us -> 4.44 us
where the time goes in v2:
time: 251 us; the launch traced here: 250 us
  waiting for transfers between devices  111 us (44%)
  Pallas kernels  88.6 us (35%)
  starting transfers between devices  44.9 us (18%)
  local copies, waits for them, and re-layouts  5.03 us (2%)
    all_to_all x4, waiting for transfers between devices, exchange(): return lax.all_to_all(value, 'seq', split_axis=0, concat_axis=0, tiled=True)  111 us
    pallas_call x2, Pallas kernels, attend(): pl.pallas_call(attend_body, in_specs=[pl.BlockSpec(memory_space=pltpu.SME...  51.4 us
    all_to_all x4, starting transfers between devices, exchange(): return lax.all_to_all(value, 'seq', split_axis=0, concat_axis=0, tiled=True)  44.9 us
    pallas_call x2, Pallas kernels, pack(): pl.pallas_call(pack_body, grid=(HEADS // COLS,), in_specs=[pl.BlockSpec(m...  31.1 us
    pallas_call x2, Pallas kernels, unpack(): pl.pallas_call(unpack_body, grid=(HEADS // COLS,), in_specs=[pl.BlockSpec...  6.17 us
  transfers between devices with their start and end apart: 4, of which 4 were waited for; matrix products, arithmetic and copies ran while one was open for 0% of the time, Pallas kernels for 23%

profile of v2, /device:TPU:1, one launch (start us, length us, event | category | flops | bytes accessed | tf_op | source)
XLA Modules:
  0.0 250.4 jit_solution(12251943995015653225)
XLA Ops:
  0.6 0.0 copy-start
  0.7 28.0 %pack0.1 = bf16[32,4,80,128]{3,2,1,0:T(8,128)(2,1)} custom-call(s32[1]{0:T(128)} %bitcast.2.wait_ref, bf16[1,2,80,4096]{3,2,1,0:T(8,128)(2,1)} %q_ref.3, bf16[1,2,80,4096]{3,2,1,0:T(8,128)(2,1)} %k_ref.3, bf16[1,2,80,4096]{3,2,1,0:T(8,128)(2,1)} %v_ref.3, bf16[1,2,80,4096]{3,2,1,0:T(8,128)(2,1)} %g_ref.3), custom_call_target="tpu_custom_call" | custom-call | bytes 5242880 | tf_op jit(solution)/shard_map/pack0/pallas_call | solution.py:33
  28.7 12.0 %all-to-all-start.2 = ((bf16[32,4,80,128]{3,2,1,0:T(8,128)(2,1)}), bf16[32,4,80,128]{3,2,1,0:T(8,128)(2,1)S(1)}, u32[]{:S(2)}, u32[]{:S(2)}) async-start(bf16[32,4,80,128]{3,2,1,0:T(8,128)(2,1)} %pack0.1), calls=%async_computation.2 | async-start | bytes 5242880 | tf_op jit(solution)/shard_map/all_to_all | solution.py:199
  40.7 3.0 %pack1.1 = bf16[32,4,80,128]{3,2,1,0:T(8,128)(2,1)} custom-call(s32[1]{0:T(128)} %constant.23.clone.1.wait_ref, bf16[1,2,80,4096]{3,2,1,0:T(8,128)(2,1)} %q_ref.3, bf16[1,2,80,4096]{3,2,1,0:T(8,128)(2,1)} %k_ref.3, bf16[1,2,80,4096]{3,2,1,0:T(8,128)(2,1)} %v_ref.3, bf16[1,2,80,4096]{3,2,1,0:T(8,128)(2,1)} %g_ref.3), custom_call_target="tpu_custom_call" | custom-call | bytes 5242880 | tf_op jit(solution)/shard_map/pack1/pallas_call | solution.py:33
  43.8 41.1 %all-to-all-done.2.x_hbm = bf16[32,4,80,128]{3,2,1,0:T(8,128)(2,1)S(1)} async-done(((bf16[32,4,80,128]{3,2,1,0:T(8,128)(2,1)}), bf16[32,4,80,128]{3,2,1,0:T(8,128)(2,1)S(1)}, u32[]{:S(2)}, u32[]{:S(2)}) %all-to-all-start.2) | async-done | bytes 2621472 | tf_op jit(solution)/shard_map/all_to_all | solution.py:199
  84.8 0.0 copy-start.3
  84.8 1.5 copy-done.3
  86.3 9.5 %all-to-all-start = ((bf16[32,4,80,128]{3,2,1,0:T(8,128)(2,1)}), bf16[32,4,80,128]{3,2,1,0:T(8,128)(2,1)S(1)}, u32[]{:S(2)}, u32[]{:S(2)}) async-start(bf16[32,4,80,128]{3,2,1,0:T(8,128)(2,1)} %pack1.1), calls=%async_computation | async-start | bytes 5242880 | tf_op jit(solution)/shard_map/all_to_all | solution.py:199
  95.8 0.0 copy-done
  95.8 0.1 constant_dynamic-slice_fusion
  95.9 0.5 fusion
  96.4 22.6 %attend0.1 = bf16[32,4,80,128]{3,2,1,0:T(8,128)(2,1)} custom-call(s32[1]{0:T(128)} %bitcast.1.len_ref, bf16[32,4,80,128]{3,2,1,0:T(8,128)(2,1)} %copy-done.3), custom_call_target="tpu_custom_call" | custom-call | flops 8388608000 | bytes 5242880 | tf_op jit(solution)/shard_map/attend0/pallas_call | solution.py:169
  119.1 18.7 %all-to-all-done.x_hbm = bf16[32,4,80,128]{3,2,1,0:T(8,128)(2,1)S(1)} async-done(((bf16[32,4,80,128]{3,2,1,0:T(8,128)(2,1)}), bf16[32,4,80,128]{3,2,1,0:T(8,128)(2,1)S(1)}, u32[]{:S(2)}, u32[]{:S(2)}) %all-to-all-start) | async-done | bytes 2621472 | tf_op jit(solution)/shard_map/all_to_all | solution.py:199
  137.8 0.0 copy-start.2
  137.8 1.5 copy-done.2
  139.3 11.6 %all-to-all-start.3 = ((bf16[32,4,80,128]{3,2,1,0:T(8,128)(2,1)}), bf16[32,4,80,128]{3,2,1,0:T(8,128)(2,1)S(1)}, u32[]{:S(2)}, u32[]{:S(2)}) async-start(bf16[32,4,80,128]{3,2,1,0:T(8,128)(2,1)} %attend0.1), calls=%async_computation.3 | async-start | bytes 5242880 | tf_op jit(solution)/shard_map/all_to_all | solution.py:199
  150.9 28.8 %attend1.1 = bf16[32,4,80,128]{3,2,1,0:T(8,128)(2,1)} custom-call(s32[1]{0:T(128)} %bitcast.len_ref, bf16[32,4,80,128]{3,2,1,0:T(8,128)(2,1)} %copy-done.2), custom_call_target="tpu_custom_call" | custom-call | flops 8388608000 | bytes 5242880 | tf_op jit(solution)/shard_map/attend1/pallas_call | solution.py:169
  179.7 12.5 %all-to-all-done.3.in_ref = bf16[32,4,80,128]{3,2,1,0:T(8,128)(2,1)S(1)} async-done(((bf16[32,4,80,128]{3,2,1,0:T(8,128)(2,1)}), bf16[32,4,80,128]{3,2,1,0:T(8,128)(2,1)S(1)}, u32[]{:S(2)}, u32[]{:S(2)}) %all-to-all-start.3) | async-done | bytes 2621472 | tf_op jit(solution)/shard_map/all_to_all | solution.py:199
  192.2 0.0 copy-start.1
  192.2 1.5 copy-done.1
  193.6 11.8 %all-to-all-start.1 = ((bf16[32,4,80,128]{3,2,1,0:T(8,128)(2,1)}), bf16[32,4,80,128]{3,2,1,0:T(8,128)(2,1)}, u32[]{:S(2)}, u32[]{:S(2)}) async-start(bf16[32,4,80,128]{3,2,1,0:T(8,128)(2,1)} %attend1.1), calls=%async_computation.1 | async-start | bytes 5242880 | tf_op jit(solution)/shard_map/all_to_all | solution.py:199
  205.4 3.1 %unpack0.1 = (bf16[1,2,80,4096]{3,2,1,0:T(8,128)(2,1)}, bf16[1,2,80,4096]{3,2,1,0:T(8,128)(2,1)}, bf16[1,2,80,4096]{3,2,1,0:T(8,128)(2,1)}, bf16[1,2,80,4096]{3,2,1,0:T(8,128)(2,1)}) custom-call(bf16[32,4,80,128]{3,2,1,0:T(8,128)(2,1)} %copy-done.1), custom_call_target="tpu_custom_call" | custom-call | bytes 5242880 | tf_op jit(solution)/shard_map/unpack0/pallas_call | solution.py:53
  208.5 38.8 %all-to-all-done.1.in_ref = bf16[32,4,80,128]{3,2,1,0:T(8,128)(2,1)} async-done(((bf16[32,4,80,128]{3,2,1,0:T(8,128)(2,1)}), bf16[32,4,80,128]{3,2,1,0:T(8,128)(2,1)}, u32[]{:S(2)}, u32[]{:S(2)}) %all-to-all-start.1) | async-done | bytes 2621472 | tf_op jit(solution)/shard_map/all_to_all | solution.py:199
  247.3 3.1 %unpack1.1 = (bf16[1,2,80,4096]{3,2,1,0:T(8,128)(2,1)}, bf16[1,2,80,4096]{3,2,1,0:T(8,128)(2,1)}, bf16[1,2,80,4096]{3,2,1,0:T(8,128)(2,1)}, bf16[1,2,80,4096]{3,2,1,0:T(8,128)(2,1)}) custom-call(bf16[32,4,80,128]{3,2,1,0:T(8,128)(2,1)} %all-to-all-done.1.in_ref, ...), custom_call_target="tpu_custom_call", output_to_operand_aliasing={{0}: (1, {}), {1}: (2, {}), {2}: (3, {}), {3}: (4, {})} | custom-call | bytes 5242880 | tf_op jit(solution)/shard_map/unpack1/pallas_call | solution.py:53
Async XLA Ops:
  0.6 95.2 %copy-start = (s32[8,2]{0,1:T(2,128)S(1)}, s32[8,2]{0,1:T(2,128)}, u32[]{:S(2)}) copy-start(s32[8,2]{0,1:T(2,128)} %param.9) | copy-start | bytes 196
  28.7 56.1 %all-to-all-start.2 = ((bf16[32,4,80,128]{3,2,1,0:T(8,128)(2,1)}), bf16[32,4,80,128]{3,2,1,0:T(8,128)(2,1)S(1)}, u32[]{:S(2)}, u32[]{:S(2)}) async-start(bf16[32,4,80,128]{3,2,1,0:T(8,128)(2,1)} %pack0.1), calls=%async_computation.2 | async-start | bytes 5242880 | tf_op jit(solution)/shard_map/all_to_all | solution.py:199
  84.8 1.5 copy-start.3
  86.3 51.5 %all-to-all-start = ((bf16[32,4,80,128]{3,2,1,0:T(8,128)(2,1)}), bf16[32,4,80,128]{3,2,1,0:T(8,128)(2,1)S(1)}, u32[]{:S(2)}, u32[]{:S(2)}) async-start(bf16[32,4,80,128]{3,2,1,0:T(8,128)(2,1)} %pack1.1), calls=%async_computation | async-start | bytes 5242880 | tf_op jit(solution)/shard_map/all_to_all | solution.py:199
  137.8 1.5 copy-start.2
  139.3 52.9 %all-to-all-start.3 = ((bf16[32,4,80,128]{3,2,1,0:T(8,128)(2,1)}), bf16[32,4,80,128]{3,2,1,0:T(8,128)(2,1)S(1)}, u32[]{:S(2)}, u32[]{:S(2)}) async-start(bf16[32,4,80,128]{3,2,1,0:T(8,128)(2,1)} %attend0.1), calls=%async_computation.3 | async-start | bytes 5242880 | tf_op jit(solution)/shard_map/all_to_all | solution.py:199
  192.2 1.5 copy-start.1
  193.6 53.7 %all-to-all-start.1 = ((bf16[32,4,80,128]{3,2,1,0:T(8,128)(2,1)}), bf16[32,4,80,128]{3,2,1,0:T(8,128)(2,1)}, u32[]{:S(2)}, u32[]{:S(2)}) async-start(bf16[32,4,80,128]{3,2,1,0:T(8,128)(2,1)} %attend1.1), calls=%async_computation.1 | async-start | bytes 5242880 | tf_op jit(solution)/shard_map/all_to_all | solution.py:199

commit v3 on v2

v3 whole, which is shorter than its diff:
```python
import functools

import jax
import jax.numpy as jnp
from jax import lax
from jax.experimental import pallas as pl
from jax.experimental.pallas import tpu as pltpu
from jax.sharding import PartitionSpec as P

HEADS = 32
HD = 128
MAX_LEN = 2560
SHARDS = 32
ROWS = MAX_LEN // SHARDS
TILE = 512
STAGGER = 24000
PARTS = 2
LOG2E = 1.4426950408889634
SCALE = HD ** (-0.5)


def pack_body(video, late_ref, q_ref, k_ref, v_ref, g_ref, out_ref, rows, held, in_sem, out_sem):
    @pl.when(late_ref[0] == 1)
    def _():
        pl.delay(STAGGER)

    wide = HEADS // PARTS
    pieces = [(a, p) for a in range(4) for p in range(PARTS)]
    refs = (q_ref, k_ref, v_ref, g_ref)

    def load(a, p):
        columns = slice(p * wide * HD, (p + 1) * wide * HD)
        return pltpu.make_async_copy(
            refs[a].at[0, video, :, columns], rows.at[a, :, columns], in_sem.at[a, p]
        )

    def store(a, p):
        heads = slice(p * wide, (p + 1) * wide)
        return pltpu.make_async_copy(held.at[heads, a], out_ref.at[heads, a], out_sem.at[a, p])

    for piece in pieces:
        load(*piece).start()
    for a, p in pieces:
        load(a, p).wait()
        for h in range(p * wide, (p + 1) * wide):
            held[h, a] = rows[a, :, h * HD : (h + 1) * HD]
        store(a, p).start()
    for piece in pieces:
        store(*piece).wait()


def pack(late, arrays, video):
    hbm = pl.BlockSpec(memory_space=pltpu.HBM)
    return pl.pallas_call(
        functools.partial(pack_body, video),
        in_specs=[pl.BlockSpec(memory_space=pltpu.SMEM)] + [hbm] * 4,
        out_specs=hbm,
        out_shape=jax.ShapeDtypeStruct((HEADS, 4, ROWS, HD), jnp.bfloat16),
        scratch_shapes=[
            pltpu.VMEM((4, ROWS, HEADS * HD), jnp.bfloat16),
            pltpu.VMEM((HEADS, 4, ROWS, HD), jnp.bfloat16),
            pltpu.SemaphoreType.DMA((4, PARTS)),
            pltpu.SemaphoreType.DMA((4, PARTS)),
        ],
        cost_estimate=pl.CostEstimate(flops=0, transcendentals=0, bytes_accessed=5242880),
        name=f"pack{video}",
    )(late, *arrays)


def unpack_body(video, count, in_ref, *refs):
    outs, (held, rows, in_sem, out_sem) = refs[count : count + 4], refs[count + 4 :]
    wide = HEADS // PARTS
    pieces = [(a, p) for a in range(4) for p in range(PARTS)]

    def load(a, p):
        heads = slice(p * wide, (p + 1) * wide)
        return pltpu.make_async_copy(in_ref.at[heads, a], held.at[heads, a], in_sem.at[a, p])

    def store(a, p):
        columns = slice(p * wide * HD, (p + 1) * wide * HD)
        return pltpu.make_async_copy(
            rows.at[a, :, columns], outs[a].at[0, video, :, columns], out_sem.at[a, p]
        )

    for piece in pieces:
        load(*piece).start()
    for a, p in pieces:
        load(a, p).wait()
        for h in range(p * wide, (p + 1) * wide):
            rows[a, :, h * HD : (h + 1) * HD] = held[h, a]
        store(a, p).start()
    for piece in pieces:
        store(*piece).wait()


def unpack(back, video, earlier):
    hbm = pl.BlockSpec(memory_space=pltpu.HBM)
    return pl.pallas_call(
        functools.partial(unpack_body, video, len(earlier)),
        in_specs=[hbm] * (1 + len(earlier)),
        out_specs=[hbm] * 4,
        out_shape=[jax.ShapeDtypeStruct((1, 2, ROWS, HEADS * HD), jnp.bfloat16)] * 4,
        input_output_aliases={1 + i: i for i in range(len(earlier))},
        scratch_shapes=[
            pltpu.VMEM((HEADS, 4, ROWS, HD), jnp.bfloat16),
            pltpu.VMEM((4, ROWS, HEADS * HD), jnp.bfloat16),
            pltpu.SemaphoreType.DMA((4, PARTS)),
            pltpu.SemaphoreType.DMA((4, PARTS)),
        ],
        cost_estimate=pl.CostEstimate(flops=0, transcendentals=0, bytes_accessed=5242880),
        name=f"unpack{video}",
    )(back, *earlier)


def dot(a, b, dims):
    return lax.dot_general(a, b, (dims, ((), ())), preferred_element_type=jnp.float32)


def attend_body(
    len_ref, x_hbm, out_hbm, x_ref, q_s, k_s, v_s, g_s, o_s, dq_s, dk_s, dv_s, sem
):
    length = len_ref[0]
    load = pltpu.make_async_copy(x_hbm, x_ref, sem)
    load.start()
    load.wait()

    def bring(s, _):
        start = pl.multiple_of(s * ROWS, ROWS)
        rows = pl.ds(start, ROWS)
        q_s[rows] = x_ref[s, 0]
        k_s[rows] = x_ref[s, 1]
        v_s[rows] = x_ref[s, 2]
        valid = lax.broadcasted_iota(jnp.int32, (ROWS, HD), 0) < length - start
        g_s[rows] = jnp.where(valid, x_ref[s, 3].astype(jnp.float32), 0.0).astype(jnp.bfloat16)
        return 0

    lax.fori_loop(0, SHARDS, bring, 0)
    o_s[...] = jnp.zeros_like(o_s)
    dq_s[...] = jnp.zeros_like(dq_s)
    dk_s[...] = jnp.zeros_like(dk_s)
    dv_s[...] = jnp.zeros_like(dv_s)
    fold = SCALE * LOG2E

    def query_tile(i, _):
        here = pl.ds(pl.multiple_of(i * TILE, TILE), TILE)
        s = dot(q_s[here], k_s[...], ((1,), (1,)))
        col = lax.broadcasted_iota(jnp.int32, (1, MAX_LEN), 1)
        s = jnp.where(col < length, s, -1e30)
        shift = jnp.max(s, axis=1, keepdims=True) * fold
        w = jnp.exp2(s * fold - shift)
        inverse = 1.0 / jnp.sum(w, axis=1, keepdims=True)
        w = w.astype(jnp.bfloat16)
        row = lax.broadcasted_iota(jnp.int32, (TILE, 1), 0) + i * TILE
        output = dot(w, v_s[...], ((1,), (0,))) * inverse
        output = jnp.where(row < length, output, 0.0).astype(jnp.bfloat16)
        o_s[here] = output
        g = g_s[here]
        delta = jnp.sum(
            g.astype(jnp.float32) * output.astype(jnp.float32), axis=1, keepdims=True
        )
        p = w.astype(jnp.float32) * inverse
        dv_s[...] += dot(p.astype(jnp.bfloat16), g, ((0,), (0,)))
        dp = dot(g, v_s[...], ((1,), (1,)))
        ds = (p * (dp - delta)).astype(jnp.bfloat16)
        dq_s[here] = (dot(ds, k_s[...], ((1,), (0,))) * SCALE).astype(jnp.bfloat16)
        dk_s[...] += dot(ds, q_s[here], ((0,), (0,)))
        return 0

    lax.fori_loop(0, (length + TILE - 1) // TILE, query_tile, 0)

    def give(s, _):
        rows = pl.ds(pl.multiple_of(s * ROWS, ROWS), ROWS)
        x_ref[s, 0] = o_s[rows]
        x_ref[s, 1] = dq_s[rows]
        x_ref[s, 2] = (dk_s[rows] * SCALE).astype(jnp.bfloat16)
        x_ref[s, 3] = dv_s[rows].astype(jnp.bfloat16)
        return 0

    lax.fori_loop(0, SHARDS, give, 0)
    store = pltpu.make_async_copy(x_ref, out_hbm, sem)
    store.start()
    store.wait()


def attend(length, received, video):
    half = pltpu.VMEM((MAX_LEN, HD), jnp.bfloat16)
    full = pltpu.VMEM((MAX_LEN, HD), jnp.float32)
    hbm = pl.BlockSpec(memory_space=pltpu.HBM)
    return pl.pallas_call(
        attend_body,
        in_specs=[pl.BlockSpec(memory_space=pltpu.SMEM), hbm],
        out_specs=hbm,
        out_shape=jax.ShapeDtypeStruct(received.shape, jnp.bfloat16),
        scratch_shapes=[pltpu.VMEM(received.shape, jnp.bfloat16)]
        + [half] * 6
        + [full, full, pltpu.SemaphoreType.DMA],
        cost_estimate=pl.CostEstimate(
            flops=10 * MAX_LEN * MAX_LEN * HD,
            transcendentals=MAX_LEN * MAX_LEN,
            bytes_accessed=4 * MAX_LEN * HD * 4,
        ),
        name=f"attend{video}",
    )(length, received)


def exchange(value):
    return lax.all_to_all(value, "seq", split_axis=0, concat_axis=0, tiled=True)


def per_device(query_rows, key_rows, value_rows, out_grad, lengths):
    arrays = (query_rows, key_rows, value_rows, out_grad)
    group = lax.axis_index("grp")
    own = lax.dynamic_index_in_dim(lengths, group, 0, keepdims=False)
    late = (group % 2).reshape(1)
    outputs = ()
    for video in range(2):
        received = exchange(pack(late * (1 - video), arrays, video))
        computed = attend(own[video : video + 1], received, video)
        outputs = unpack(exchange(computed), video, outputs)
    return tuple(outputs)


def solution(mesh):
    rows = P("grp", None, "seq", None)
    return jax.shard_map(
        per_device,
        mesh=mesh,
        in_specs=(rows, rows, rows, rows, P()),
        out_specs=(rows, rows, rows, rows),
        check_vma=False,
    )
```

time: 251 us -> 251 us (level)
    pallas_call x4, Pallas kernels: 37.2 us -> 34.7 us  [the longest x2 29.4 us: pack(): pl.pallas_call(functools.partial(pack_body, video), in_specs=[pl.BlockSpe...]
where the time goes in v3:
time: 251 us; the launch traced here: 250 us
  waiting for transfers between devices  113 us (45%)
  Pallas kernels  86.5 us (34%)
  starting transfers between devices  45.1 us (18%)
  local copies, waits for them, and re-layouts  5.03 us (2%)
    all_to_all x4, waiting for transfers between devices, exchange(): return lax.all_to_all(value, 'seq', split_axis=0, concat_axis=0, tiled=True)  113 us
    pallas_call x2, Pallas kernels, attend(): pl.pallas_call(attend_body, in_specs=[pl.BlockSpec(memory_space=pltpu.SME...  51.7 us
    all_to_all x4, starting transfers between devices, exchange(): return lax.all_to_all(value, 'seq', split_axis=0, concat_axis=0, tiled=True)  45.1 us
    pallas_call x2, Pallas kernels, pack(): pl.pallas_call(functools.partial(pack_body, video), in_specs=[pl.BlockSpe...  29.4 us
    pallas_call x2, Pallas kernels, unpack(): pl.pallas_call(functools.partial(unpack_body, video, len(earlier)), in_sp...  5.32 us
  transfers between devices with their start and end apart: 4, of which 4 were waited for; matrix products, arithmetic and copies ran while one was open for 0% of the time, Pallas kernels for 23%

profile of v3, /device:TPU:1, one launch (start us, length us, event | category | flops | bytes accessed | tf_op | source)
XLA Modules:
  0.0 250.0 jit_solution(6370148982760296935)
XLA Ops:
  0.6 0.0 copy-start
  0.7 26.7 %pack0.1 = bf16[32,4,80,128]{3,2,1,0:T(8,128)(2,1)} custom-call(s32[1]{0:T(128)} %bitcast.2.late_ref, bf16[1,2,80,4096]{3,2,1,0:T(8,128)(2,1)} %q_ref.3, bf16[1,2,80,4096]{3,2,1,0:T(8,128)(2,1)} %k_ref.3, bf16[1,2,80,4096]{3,2,1,0:T(8,128)(2,1)} %v_ref.3, bf16[1,2,80,4096]{3,2,1,0:T(8,128)(2,1)} %g_ref.3), custom_call_target="tpu_custom_call" | custom-call | bytes 5242880 | tf_op jit(solution)/shard_map/pack0/pallas_call | solution.py:54
  27.4 12.0 %all-to-all-start.2 = ((bf16[32,4,80,128]{3,2,1,0:T(8,128)(2,1)}), bf16[32,4,80,128]{3,2,1,0:T(8,128)(2,1)S(1)}, u32[]{:S(2)}, u32[]{:S(2)}) async-start(bf16[32,4,80,128]{3,2,1,0:T(8,128)(2,1)} %pack0.1), calls=%async_computation.2 | async-start | bytes 5242880 | tf_op jit(solution)/shard_map/all_to_all | solution.py:207
  39.4 2.7 %pack1.1 = bf16[32,4,80,128]{3,2,1,0:T(8,128)(2,1)} custom-call(s32[1]{0:T(128)} %constant.23.clone.1.late_ref, bf16[1,2,80,4096]{3,2,1,0:T(8,128)(2,1)} %q_ref.3, bf16[1,2,80,4096]{3,2,1,0:T(8,128)(2,1)} %k_ref.3, bf16[1,2,80,4096]{3,2,1,0:T(8,128)(2,1)} %v_ref.3, bf16[1,2,80,4096]{3,2,1,0:T(8,128)(2,1)} %g_ref.3), custom_call_target="tpu_custom_call" | custom-call | bytes 5242880 | tf_op jit(solution)/shard_map/pack1/pallas_call | solution.py:54
  42.1 39.6 %all-to-all-done.2.x_hbm = bf16[32,4,80,128]{3,2,1,0:T(8,128)(2,1)S(1)} async-done(((bf16[32,4,80,128]{3,2,1,0:T(8,128)(2,1)}), bf16[32,4,80,128]{3,2,1,0:T(8,128)(2,1)S(1)}, u32[]{:S(2)}, u32[]{:S(2)}) %all-to-all-start.2) | async-done | bytes 2621472 | tf_op jit(solution)/shard_map/all_to_all | solution.py:207
  81.7 0.0 copy-start.3
  81.7 1.5 copy-done.3
  83.2 11.1 %all-to-all-start = ((bf16[32,4,80,128]{3,2,1,0:T(8,128)(2,1)}), bf16[32,4,80,128]{3,2,1,0:T(8,128)(2,1)S(1)}, u32[]{:S(2)}, u32[]{:S(2)}) async-start(bf16[32,4,80,128]{3,2,1,0:T(8,128)(2,1)} %pack1.1), calls=%async_computation | async-start | bytes 5242880 | tf_op jit(solution)/shard_map/all_to_all | solution.py:207
  94.3 0.0 copy-done
  94.3 0.1 constant_dynamic-slice_fusion
  94.4 0.5 fusion
  94.9 31.0 %attend0.1 = bf16[32,4,80,128]{3,2,1,0:T(8,128)(2,1)} custom-call(s32[1]{0:T(128)} %bitcast.1.len_ref, bf16[32,4,80,128]{3,2,1,0:T(8,128)(2,1)} %copy-done.3), custom_call_target="tpu_custom_call" | custom-call | flops 8388608000 | bytes 5242880 | tf_op jit(solution)/shard_map/attend0/pallas_call | solution.py:189
  125.9 10.4 %all-to-all-done.x_hbm = bf16[32,4,80,128]{3,2,1,0:T(8,128)(2,1)S(1)} async-done(((bf16[32,4,80,128]{3,2,1,0:T(8,128)(2,1)}), bf16[32,4,80,128]{3,2,1,0:T(8,128)(2,1)S(1)}, u32[]{:S(2)}, u32[]{:S(2)}) %all-to-all-start) | async-done | bytes 2621472 | tf_op jit(solution)/shard_map/all_to_all | solution.py:207
  136.3 0.0 copy-start.2
  136.3 1.5 copy-done.2
  137.8 12.0 %all-to-all-start.3 = ((bf16[32,4,80,128]{3,2,1,0:T(8,128)(2,1)}), bf16[32,4,80,128]{3,2,1,0:T(8,128)(2,1)S(1)}, u32[]{:S(2)}, u32[]{:S(2)}) async-start(bf16[32,4,80,128]{3,2,1,0:T(8,128)(2,1)} %attend0.1), calls=%async_computation.3 | async-start | bytes 5242880 | tf_op jit(solution)/shard_map/all_to_all | solution.py:207
  149.8 20.8 %attend1.1 = bf16[32,4,80,128]{3,2,1,0:T(8,128)(2,1)} custom-call(s32[1]{0:T(128)} %bitcast.len_ref, bf16[32,4,80,128]{3,2,1,0:T(8,128)(2,1)} %copy-done.2), custom_call_target="tpu_custom_call" | custom-call | flops 8388608000 | bytes 5242880 | tf_op jit(solution)/shard_map/attend1/pallas_call | solution.py:189
  170.6 22.0 %all-to-all-done.3.in_ref = bf16[32,4,80,128]{3,2,1,0:T(8,128)(2,1)S(1)} async-done(((bf16[32,4,80,128]{3,2,1,0:T(8,128)(2,1)}), bf16[32,4,80,128]{3,2,1,0:T(8,128)(2,1)S(1)}, u32[]{:S(2)}, u32[]{:S(2)}) %all-to-all-start.3) | async-done | bytes 2621472 | tf_op jit(solution)/shard_map/all_to_all | solution.py:207
  192.6 0.0 copy-start.1
  192.6 1.5 copy-done.1
  194.1 9.9 %all-to-all-start.1 = ((bf16[32,4,80,128]{3,2,1,0:T(8,128)(2,1)}), bf16[32,4,80,128]{3,2,1,0:T(8,128)(2,1)}, u32[]{:S(2)}, u32[]{:S(2)}) async-start(bf16[32,4,80,128]{3,2,1,0:T(8,128)(2,1)} %attend1.1), calls=%async_computation.1 | async-start | bytes 5242880 | tf_op jit(solution)/shard_map/all_to_all | solution.py:207
  204.0 2.7 %unpack0.1 = (bf16[1,2,80,4096]{3,2,1,0:T(8,128)(2,1)}, bf16[1,2,80,4096]{3,2,1,0:T(8,128)(2,1)}, bf16[1,2,80,4096]{3,2,1,0:T(8,128)(2,1)}, bf16[1,2,80,4096]{3,2,1,0:T(8,128)(2,1)}) custom-call(bf16[32,4,80,128]{3,2,1,0:T(8,128)(2,1)} %copy-done.1), custom_call_target="tpu_custom_call" | custom-call | bytes 5242880 | tf_op jit(solution)/shard_map/unpack0/pallas_call | solution.py:98
  206.7 40.5 %all-to-all-done.1.in_ref = bf16[32,4,80,128]{3,2,1,0:T(8,128)(2,1)} async-done(((bf16[32,4,80,128]{3,2,1,0:T(8,128)(2,1)}), bf16[32,4,80,128]{3,2,1,0:T(8,128)(2,1)}, u32[]{:S(2)}, u32[]{:S(2)}) %all-to-all-start.1) | async-done | bytes 2621472 | tf_op jit(solution)/shard_map/all_to_all | solution.py:207
  247.2 2.7 %unpack1.1 = (bf16[1,2,80,4096]{3,2,1,0:T(8,128)(2,1)}, bf16[1,2,80,4096]{3,2,1,0:T(8,128)(2,1)}, bf16[1,2,80,4096]{3,2,1,0:T(8,128)(2,1)}, bf16[1,2,80,4096]{3,2,1,0:T(8,128)(2,1)}) custom-call(bf16[32,4,80,128]{3,2,1,0:T(8,128)(2,1)} %all-to-all-done.1.in_ref, ...), custom_call_target="tpu_custom_call", output_to_operand_aliasing={{0}: (1, {}), {1}: (2, {}), {2}: (3, {}), {3}: (4, {})} | custom-call | bytes 5242880 | tf_op jit(solution)/shard_map/unpack1/pallas_call | solution.py:98
Async XLA Ops:
  0.6 93.7 %copy-start = (s32[8,2]{0,1:T(2,128)S(1)}, s32[8,2]{0,1:T(2,128)}, u32[]{:S(2)}) copy-start(s32[8,2]{0,1:T(2,128)} %param.9) | copy-start | bytes 196
  27.4 54.4 %all-to-all-start.2 = ((bf16[32,4,80,128]{3,2,1,0:T(8,128)(2,1)}), bf16[32,4,80,128]{3,2,1,0:T(8,128)(2,1)S(1)}, u32[]{:S(2)}, u32[]{:S(2)}) async-start(bf16[32,4,80,128]{3,2,1,0:T(8,128)(2,1)} %pack0.1), calls=%async_computation.2 | async-start | bytes 5242880 | tf_op jit(solution)/shard_map/all_to_all | solution.py:207
  81.7 1.5 copy-start.3
  83.2 53.1 %all-to-all-start = ((bf16[32,4,80,128]{3,2,1,0:T(8,128)(2,1)}), bf16[32,4,80,128]{3,2,1,0:T(8,128)(2,1)S(1)}, u32[]{:S(2)}, u32[]{:S(2)}) async-start(bf16[32,4,80,128]{3,2,1,0:T(8,128)(2,1)} %pack1.1), calls=%async_computation | async-start | bytes 5242880 | tf_op jit(solution)/shard_map/all_to_all | solution.py:207
  136.3 1.5 copy-start.2
  137.8 54.8 %all-to-all-start.3 = ((bf16[32,4,80,128]{3,2,1,0:T(8,128)(2,1)}), bf16[32,4,80,128]{3,2,1,0:T(8,128)(2,1)S(1)}, u32[]{:S(2)}, u32[]{:S(2)}) async-start(bf16[32,4,80,128]{3,2,1,0:T(8,128)(2,1)} %attend0.1), calls=%async_computation.3 | async-start | bytes 5242880 | tf_op jit(solution)/shard_map/all_to_all | solution.py:207
  192.6 1.5 copy-start.1
  194.1 53.1 %all-to-all-start.1 = ((bf16[32,4,80,128]{3,2,1,0:T(8,128)(2,1)}), bf16[32,4,80,128]{3,2,1,0:T(8,128)(2,1)}, u32[]{:S(2)}, u32[]{:S(2)}) async-start(bf16[32,4,80,128]{3,2,1,0:T(8,128)(2,1)} %attend1.1), calls=%async_computation.1 | async-start | bytes 5242880 | tf_op jit(solution)/shard_map/all_to_all | solution.py:207

commit v4 on v3

--- a/solution.py
+++ b/solution.py
@@ -15,6 +15,7 @@
 TILE = 512
 STAGGER = 24000
 PARTS = 2
+VMEM = 67043328
 LOG2E = 1.4426950408889634
 SCALE = HD ** (-0.5)
 
@@ -62,6 +63,7 @@
             pltpu.SemaphoreType.DMA((4, PARTS)),
             pltpu.SemaphoreType.DMA((4, PARTS)),
         ],
+        compiler_params=pltpu.CompilerParams(vmem_limit_bytes=VMEM),
         cost_estimate=pl.CostEstimate(flops=0, transcendentals=0, bytes_accessed=5242880),
         name=f"pack{video}",
     )(late, *arrays)
@@ -107,6 +109,7 @@
             pltpu.SemaphoreType.DMA((4, PARTS)),
             pltpu.SemaphoreType.DMA((4, PARTS)),
         ],
+        compiler_params=pltpu.CompilerParams(vmem_limit_bytes=VMEM),
         cost_estimate=pl.CostEstimate(flops=0, transcendentals=0, bytes_accessed=5242880),
         name=f"unpack{video}",
     )(back, *earlier)
@@ -194,6 +197,7 @@
         scratch_shapes=[pltpu.VMEM(received.shape, jnp.bfloat16)]
         + [half] * 6
         + [full, full, pltpu.SemaphoreType.DMA],
+        compiler_params=pltpu.CompilerParams(vmem_limit_bytes=VMEM),
         cost_estimate=pl.CostEstimate(
             flops=10 * MAX_LEN * MAX_LEN * HD,
             transcendentals=MAX_LEN * MAX_LEN,

time: 251 us -> 252 us (level)
  Pallas kernels: 86.5 us -> 96.8 us
  local copies, waits for them, and re-layouts: 5.03 us -> 0.6 us
  starting transfers between devices: 45.1 us -> 40.9 us
    pallas_call x2, Pallas kernels: 51.7 us -> 62 us  [attend(): pl.pallas_call(attend_body, in_specs=[pl.BlockSpec(memory_space=pltpu.SME...]
    unnamed x8 -> x2, local copies, waits for them, and re-layouts: 4.44 us -> 0.01 us
    all_to_all x4, starting transfers between devices: 45.1 us -> 40.9 us  [exchange(): return lax.all_to_all(value, 'seq', split_axis=0, concat_axis=0, tiled=True)]
  transfers between devices with their start and end apart: 4 -> 4, of which waited for: 4 -> 4; matrix products, arithmetic and copies ran while one was open for 0% -> 0% of each run, Pallas kernels for 23% -> 27%
where the time goes in v4:
time: 252 us; the launch traced here: 251 us
  waiting for transfers between devices  112 us (44%)
  Pallas kernels  96.8 us (38%)
  starting transfers between devices  40.9 us (16%)
    all_to_all x4, waiting for transfers between devices, exchange(): return lax.all_to_all(value, 'seq', split_axis=0, concat_axis=0, tiled=True)  112 us
    pallas_call x2, Pallas kernels, attend(): pl.pallas_call(attend_body, in_specs=[pl.BlockSpec(memory_space=pltpu.SME...  62 us
    all_to_all x4, starting transfers between devices, exchange(): return lax.all_to_all(value, 'seq', split_axis=0, concat_axis=0, tiled=True)  40.9 us
    pallas_call x2, Pallas kernels, pack(): pl.pallas_call(functools.partial(pack_body, video), in_specs=[pl.BlockSpe...  29.4 us
    pallas_call x2, Pallas kernels, unpack(): pl.pallas_call(functools.partial(unpack_body, video, len(earlier)), in_sp...  5.32 us
  transfers between devices with their start and end apart: 4, of which 4 were waited for; matrix products, arithmetic and copies ran while one was open for 0% of the time, Pallas kernels for 27%

profile of v4, /device:TPU:1, one launch (start us, length us, event | category | flops | bytes accessed | tf_op | source)
XLA Modules:
  0.0 250.9 jit_solution(36794027460939692)
XLA Ops:
  0.6 26.7 %pack0.1 = bf16[32,4,80,128]{3,2,1,0:T(8,128)(2,1)} custom-call(s32[1]{0:T(128)} %bitcast.2.late_ref, bf16[1,2,80,4096]{3,2,1,0:T(8,128)(2,1)} %q_ref.3, bf16[1,2,80,4096]{3,2,1,0:T(8,128)(2,1)} %k_ref.3, bf16[1,2,80,4096]{3,2,1,0:T(8,128)(2,1)} %v_ref.3, bf16[1,2,80,4096]{3,2,1,0:T(8,128)(2,1)} %g_ref.3), custom_call_target="tpu_custom_call" | custom-call | bytes 5242880 | tf_op jit(solution)/shard_map/pack0/pallas_call | solution.py:55
  27.3 12.2 %all-to-all-start.2 = ((bf16[32,4,80,128]{3,2,1,0:T(8,128)(2,1)}), bf16[32,4,80,128]{3,2,1,0:T(8,128)(2,1)}, u32[]{:S(2)}, u32[]{:S(2)}) async-start(bf16[32,4,80,128]{3,2,1,0:T(8,128)(2,1)} %pack0.1), calls=%async_computation.2 | async-start | bytes 5242880 | tf_op jit(solution)/shard_map/all_to_all | solution.py:211
  39.5 2.7 %pack1.1 = bf16[32,4,80,128]{3,2,1,0:T(8,128)(2,1)} custom-call(s32[1]{0:T(128)} %constant.23.clone.1.late_ref, bf16[1,2,80,4096]{3,2,1,0:T(8,128)(2,1)} %q_ref.3, bf16[1,2,80,4096]{3,2,1,0:T(8,128)(2,1)} %k_ref.3, bf16[1,2,80,4096]{3,2,1,0:T(8,128)(2,1)} %v_ref.3, bf16[1,2,80,4096]{3,2,1,0:T(8,128)(2,1)} %g_ref.3), custom_call_target="tpu_custom_call" | custom-call | bytes 5242880 | tf_op jit(solution)/shard_map/pack1/pallas_call | solution.py:55
  42.2 0.0 copy-start
  42.2 41.5 %all-to-all-done.2.x_hbm = bf16[32,4,80,128]{3,2,1,0:T(8,128)(2,1)} async-done(((bf16[32,4,80,128]{3,2,1,0:T(8,128)(2,1)}), bf16[32,4,80,128]{3,2,1,0:T(8,128)(2,1)}, u32[]{:S(2)}, u32[]{:S(2)}) %all-to-all-start.2) | async-done | bytes 2621472 | tf_op jit(solution)/shard_map/all_to_all | solution.py:211
  83.8 9.9 %all-to-all-start = ((bf16[32,4,80,128]{3,2,1,0:T(8,128)(2,1)}), bf16[32,4,80,128]{3,2,1,0:T(8,128)(2,1)}, u32[]{:S(2)}, u32[]{:S(2)}) async-start(bf16[32,4,80,128]{3,2,1,0:T(8,128)(2,1)} %pack1.1), calls=%async_computation | async-start | bytes 5242880 | tf_op jit(solution)/shard_map/all_to_all | solution.py:211
  93.7 0.0 copy-done
  93.7 0.1 constant_dynamic-slice_fusion
  93.8 0.5 fusion
  94.3 30.9 %attend0.1 = bf16[32,4,80,128]{3,2,1,0:T(8,128)(2,1)} custom-call(s32[1]{0:T(128)} %bitcast.1.len_ref, bf16[32,4,80,128]{3,2,1,0:T(8,128)(2,1)} %all-to-all-done.2.x_hbm), custom_call_target="tpu_custom_call" | custom-call | flops 8388608000 | bytes 5242880 | tf_op jit(solution)/shard_map/attend0/pallas_call | solution.py:192
  125.2 15.4 %all-to-all-done.x_hbm = bf16[32,4,80,128]{3,2,1,0:T(8,128)(2,1)} async-done(((bf16[32,4,80,128]{3,2,1,0:T(8,128)(2,1)}), bf16[32,4,80,128]{3,2,1,0:T(8,128)(2,1)}, u32[]{:S(2)}, u32[]{:S(2)}) %all-to-all-start) | async-done | bytes 2621472 | tf_op jit(solution)/shard_map/all_to_all | solution.py:211
  140.6 8.6 %all-to-all-start.3 = ((bf16[32,4,80,128]{3,2,1,0:T(8,128)(2,1)}), bf16[32,4,80,128]{3,2,1,0:T(8,128)(2,1)}, u32[]{:S(2)}, u32[]{:S(2)}) async-start(bf16[32,4,80,128]{3,2,1,0:T(8,128)(2,1)} %attend0.1), calls=%async_computation.3 | async-start | bytes 5242880 | tf_op jit(solution)/shard_map/all_to_all | solution.py:211
  149.2 31.1 %attend1.1 = bf16[32,4,80,128]{3,2,1,0:T(8,128)(2,1)} custom-call(s32[1]{0:T(128)} %bitcast.len_ref, bf16[32,4,80,128]{3,2,1,0:T(8,128)(2,1)} %all-to-all-done.x_hbm), custom_call_target="tpu_custom_call" | custom-call | flops 8388608000 | bytes 5242880 | tf_op jit(solution)/shard_map/attend1/pallas_call | solution.py:192
  180.4 11.8 %all-to-all-done.3.in_ref = bf16[32,4,80,128]{3,2,1,0:T(8,128)(2,1)} async-done(((bf16[32,4,80,128]{3,2,1,0:T(8,128)(2,1)}), bf16[32,4,80,128]{3,2,1,0:T(8,128)(2,1)}, u32[]{:S(2)}, u32[]{:S(2)}) %all-to-all-start.3) | async-done | bytes 2621472 | tf_op jit(solution)/shard_map/all_to_all | solution.py:211
  192.2 10.2 %all-to-all-start.1 = ((bf16[32,4,80,128]{3,2,1,0:T(8,128)(2,1)}), bf16[32,4,80,128]{3,2,1,0:T(8,128)(2,1)}, u32[]{:S(2)}, u32[]{:S(2)}) async-start(bf16[32,4,80,128]{3,2,1,0:T(8,128)(2,1)} %attend1.1), calls=%async_computation.1 | async-start | bytes 5242880 | tf_op jit(solution)/shard_map/all_to_all | solution.py:211
  202.4 2.7 %unpack0.1 = (bf16[1,2,80,4096]{3,2,1,0:T(8,128)(2,1)}, bf16[1,2,80,4096]{3,2,1,0:T(8,128)(2,1)}, bf16[1,2,80,4096]{3,2,1,0:T(8,128)(2,1)}, bf16[1,2,80,4096]{3,2,1,0:T(8,128)(2,1)}) custom-call(bf16[32,4,80,128]{3,2,1,0:T(8,128)(2,1)} %all-to-all-done.3.in_ref), custom_call_target="tpu_custom_call" | custom-call | bytes 5242880 | tf_op jit(solution)/shard_map/unpack0/pallas_call | solution.py:100
  205.1 43.0 %all-to-all-done.1.in_ref = bf16[32,4,80,128]{3,2,1,0:T(8,128)(2,1)} async-done(((bf16[32,4,80,128]{3,2,1,0:T(8,128)(2,1)}), bf16[32,4,80,128]{3,2,1,0:T(8,128)(2,1)}, u32[]{:S(2)}, u32[]{:S(2)}) %all-to-all-start.1) | async-done | bytes 2621472 | tf_op jit(solution)/shard_map/all_to_all | solution.py:211
  248.1 2.7 %unpack1.1 = (bf16[1,2,80,4096]{3,2,1,0:T(8,128)(2,1)}, bf16[1,2,80,4096]{3,2,1,0:T(8,128)(2,1)}, bf16[1,2,80,4096]{3,2,1,0:T(8,128)(2,1)}, bf16[1,2,80,4096]{3,2,1,0:T(8,128)(2,1)}) custom-call(bf16[32,4,80,128]{3,2,1,0:T(8,128)(2,1)} %all-to-all-done.1.in_ref, ...), custom_call_target="tpu_custom_call", output_to_operand_aliasing={{0}: (1, {}), {1}: (2, {}), {2}: (3, {}), {3}: (4, {})} | custom-call | bytes 5242880 | tf_op jit(solution)/shard_map/unpack1/pallas_call | solution.py:100
Async XLA Ops:
  27.3 56.4 %all-to-all-start.2 = ((bf16[32,4,80,128]{3,2,1,0:T(8,128)(2,1)}), bf16[32,4,80,128]{3,2,1,0:T(8,128)(2,1)}, u32[]{:S(2)}, u32[]{:S(2)}) async-start(bf16[32,4,80,128]{3,2,1,0:T(8,128)(2,1)} %pack0.1), calls=%async_computation.2 | async-start | bytes 5242880 | tf_op jit(solution)/shard_map/all_to_all | solution.py:211
  42.2 51.5 %copy-start = (s32[8,2]{0,1:T(2,128)S(1)}, s32[8,2]{0,1:T(2,128)}, u32[]{:S(2)}) copy-start(s32[8,2]{0,1:T(2,128)} %param.9) | copy-start | bytes 196
  83.8 56.8 %all-to-all-start = ((bf16[32,4,80,128]{3,2,1,0:T(8,128)(2,1)}), bf16[32,4,80,128]{3,2,1,0:T(8,128)(2,1)}, u32[]{:S(2)}, u32[]{:S(2)}) async-start(bf16[32,4,80,128]{3,2,1,0:T(8,128)(2,1)} %pack1.1), calls=%async_computation | async-start | bytes 5242880 | tf_op jit(solution)/shard_map/all_to_all | solution.py:211
  140.6 51.6 %all-to-all-start.3 = ((bf16[32,4,80,128]{3,2,1,0:T(8,128)(2,1)}), bf16[32,4,80,128]{3,2,1,0:T(8,128)(2,1)}, u32[]{:S(2)}, u32[]{:S(2)}) async-start(bf16[32,4,80,128]{3,2,1,0:T(8,128)(2,1)} %attend0.1), calls=%async_computation.3 | async-start | bytes 5242880 | tf_op jit(solution)/shard_map/all_to_all | solution.py:211
  192.2 55.9 %all-to-all-start.1 = ((bf16[32,4,80,128]{3,2,1,0:T(8,128)(2,1)}), bf16[32,4,80,128]{3,2,1,0:T(8,128)(2,1)}, u32[]{:S(2)}, u32[]{:S(2)}) async-start(bf16[32,4,80,128]{3,2,1,0:T(8,128)(2,1)} %attend1.1), calls=%async_computation.1 | async-start | bytes 5242880 | tf_op jit(solution)/shard_map/all_to_all | solution.py:211
